TPU v7x, 32 devices: a whole 2x2x4 slice. The times are simulated.
32 devices in a mesh: aux: 4 (over y, x), blk: 4 (over z), occ: 2 (over core).
Axes of the slice: x: 2, y: 2, z: 4, core: 2. Of those that a mesh axis runs over, the one named last changes fastest.
Arguments:
- integrals: bfloat16 [16, 4, 11, 512, 512], P('aux', 'blk'), may hold values from -0.078125 to 0.078125
- orbitals: bfloat16 [2048, 512], P('blk', 'occ'), may hold values from -6 to 6
- pair_lists: int32 [4, 11], P('blk'), may hold values from 0 to 3, as said below
- pair_counts: int32 [4], P('blk'), may hold values from 1 to 11, as said below
Outputs:
- exchange: float32 [4, 512, 512], P('blk', 'aux')
Inputs may be any that keep to these rules, and one draw needn't show every extreme that they name: `pair_lists`: entry 0 of row m is m itself; entries past pair_counts[m] are never read. `pair_counts`: some block has all 11 slots live.
All inputs are finite; a program needn't handle non-finite values.
Results may differ from a plain program's by a relative error of at most 0.00099.
Values may be sent and summed in bfloat16 or wider, within the bound.
No kernel may reach another device: no remote copies, remote signals or barrier semaphores. Data moves between devices by JAX's collectives and lax.ppermute only.
A program may use at most 192 MiB of HBM per device.

v0:
```python
import functools
import math

import jax
import jax.numpy as jnp
from jax import lax
from jax.experimental import pallas as pl
from jax.experimental.pallas import tpu as pltpu
from jax.sharding import PartitionSpec as P


ANY = pl.BlockSpec(memory_space=pl.ANY)
VMEM = pl.BlockSpec(memory_space=pltpu.VMEM)
SMEM = pl.BlockSpec(memory_space=pltpu.SMEM)
HBM = pl.BlockSpec(memory_space=pltpu.HBM)


SCALED_TOP = 14
EXPONENT_ROWS = 16


def exchange_pairs(distance, size):
    return [(i, i ^ distance) for i in range(size)]


def mirrored(value, size, core):
    bits = size.bit_length() - 1
    other = sum(((value >> i) & 1) << (bits - 1 - i) for i in range(bits))
    if isinstance(core, int):
        return other if core % 2 else value
    return jnp.where(core % 2 == 1, other, value)


def my_seat():
    return mirrored(lax.axis_index("aux"), lax.axis_size("aux"), lax.axis_index("occ"))


def aux_exchange(distance, aux_size, occ_size):
    return [
        (a * occ_size + c, (a ^ mirrored(distance, aux_size, c)) * occ_size + c)
        for a in range(aux_size)
        for c in range(occ_size)
    ]


def in_hbm(x):
    return pltpu.with_memory_space_constraint(x, pltpu.HBM)


def slot_product(block, coef):
    aux_total, width, _ = block.shape
    product = jnp.dot(
        block.reshape(aux_total * width, width), coef, preferred_element_type=jnp.float32
    )
    return product.reshape(aux_total, width, coef.shape[1])


def add_slots(table, group, ints_ref, coef_rows, acc_ref, fresh=False):
    begin, end = group_bounds(table, group, ints_ref.shape[2])

    def product(i):
        return slot_product(ints_ref[:, 0, table[i]], coef_rows(i))

    if fresh:
        acc_ref[...] = product(0)
        begin = 1
    pairs = (end - begin) // 2

    @pl.loop(0, pairs)
    def _(pair):
        i = begin + 2 * pair
        acc_ref[...] += product(i) + product(i + 1)

    @pl.when(begin + 2 * pairs < end)
    def _():
        acc_ref[...] += product(end - 1)


def group_bounds(table, group, slot_total):
    ends = 2 * slot_total + 2
    return (table[ends + group - 1] if group else 0), table[ends + group]


def head_kernel(piece, t, coef_hbm, out_ref, sem):
    width = coef_hbm.shape[0]
    depth = (lax.axis_size("blk") - 2) * width // lax.axis_size("aux")
    start = lax.rem(my_seat() * depth + t * piece, width)
    rows = pl.ds(pl.multiple_of(start, piece), piece)
    copy = pltpu.make_async_copy(coef_hbm.at[rows], out_ref, sem)
    copy.start()
    copy.wait()


def sort_kernel(far_depth, width, counts, lists, table):
    slot_total = lists.shape[1]
    me, seat = lax.axis_index("blk"), my_seat()
    live = counts[0]
    piece = math.gcd(far_depth, width)
    groups, sizes = [], [jnp.int32(0)] * 4
    for slot in range(slot_total):
        away = lists[0, slot] ^ me
        last = jnp.int32(0)
        for part in range(width // piece):
            last = jnp.maximum(last, lax.div((away - 2) * width + part * piece, far_depth) ^ seat)
        far_group = jnp.where(last <= 1, 2, 3)
        groups.append(jnp.where(slot < live, jnp.where(away < 2, away, far_group), 4))
        sizes = [n + (groups[-1] == g).astype(jnp.int32) for g, n in enumerate(sizes)]
    cursors, found = [], jnp.int32(0)
    for group, size in enumerate(sizes):
        cursors.append(found)
        found = found + size
        table[2 * slot_total + 2 + group] = found
    for slot in range(slot_total):
        place = jnp.int32(slot_total)
        for group in range(4):
            place = jnp.where(groups[slot] == group, cursors[group], place)
        cursors = [n + (groups[slot] == g).astype(jnp.int32) for g, n in enumerate(cursors)]
        table[place] = slot
        table[slot_total + 1 + place] = lists[0, slot] ^ me


def near_kernel(group, table, ints_ref, coef_ref, *accs):
    add_slots(table, group, ints_ref, lambda i: coef_ref[...], accs[-1], fresh=group == 0)


def add_far(group, needed, table, ints_ref, chunks, coef, acc_ref):
    _, _, slot_total, width, _ = ints_ref.shape
    depth = chunks[0].shape[0]
    me = my_seat()
    for k in needed:
        rows = pl.ds(pl.multiple_of((me ^ k) * depth, depth), depth)
        coef[rows, :] = chunks[k][...]

    def coef_rows(i):
        start = (table[slot_total + 1 + i] - 2) * width
        return coef[pl.ds(pl.multiple_of(start, width), width), :]

    add_slots(table, group, ints_ref, coef_rows, acc_ref)


def far_kernel(needed, table, ints_ref, *rest):
    *chunks, _, acc_ref, coef = rest
    add_far(2, needed, table, ints_ref, chunks, coef, acc_ref)


def last_kernel(needed, occ_size, table, ints_ref, *rest):
    *chunks, _, acc_ref, halves = rest[: -occ_size]
    pieces, coef = rest[-occ_size:-1], rest[-1]
    add_far(3, needed, table, ints_ref, chunks, coef, acc_ref)
    columns = acc_ref.shape[2]
    for p in range(acc_ref.shape[0]):
        halves[:, p * columns : (p + 1) * columns] = acc_ref[p].astype(jnp.bfloat16)
    for k, piece_ref in enumerate(pieces, 1):
        share_kernel(k, halves, piece_ref)


def share_kernel(distance, halves, piece_ref):
    share = piece_ref.shape[1]
    start = (lax.axis_index("occ") ^ distance) * share
    rows = pl.ds(pl.multiple_of(start, share), share)
    piece_ref[...] = lax.dot_general(
        halves[...], halves[rows, :], (((1,), (1,)), ((), ())), preferred_element_type=jnp.float32
    )


def split_kernel(*refs):
    aux_size, occ_size = lax.axis_size("aux"), lax.axis_size("occ")
    terms, outs = refs[:occ_size], refs[occ_size:]
    my_aux, my_occ = lax.axis_index("aux"), lax.axis_index("occ")
    depth = outs[0].shape[0]
    for k in range(aux_size):
        target = my_aux ^ mirrored(k, aux_size, my_occ)
        rows = pl.ds(pl.multiple_of(target * depth, depth), depth)
        total = terms[0][rows, :]
        for term in terms[1:]:
            total = total + term[rows, :]
        if k == 0:
            outs[k][...] = total
            continue
        peak = jnp.max(jnp.abs(total), axis=0, keepdims=True)
        exponent = jnp.ceil(jnp.log(jnp.maximum(peak, 2.0**-100)) * (1 / math.log(2.0)))
        outs[k][:depth, :] = total * jnp.exp2(SCALED_TOP - exponent)
        outs[k][depth:, :] = jnp.broadcast_to(exponent, (EXPONENT_ROWS, total.shape[1]))


def unscaled(block, depth):
    block = block.astype(jnp.float32)
    return block[:depth] * jnp.exp2(block[depth : depth + 1] - SCALED_TOP)


def per_device(integrals, orbitals, pair_lists, pair_counts):
    aux_total, _, slot_total, width, _ = integrals.shape
    columns = orbitals.shape[1]
    aux_size, blk_size, occ_size = (lax.axis_size(n) for n in ("aux", "blk", "occ"))
    my_occ = lax.axis_index("occ")
    slot_flops = 2 * aux_total * width * width * columns
    slot_bytes = 2 * aux_total * width * width

    def cost(slots):
        return pl.CostEstimate(
            flops=slots * slot_flops, bytes_accessed=slots * slot_bytes, transcendentals=0
        )

    depth = (blk_size - 2) * width // aux_size
    piece = math.gcd(depth, width)
    parts = []
    for t in range(depth // piece):
        pairs = []
        for a in range(aux_size):
            for c in range(occ_size):
                away = 2 + (mirrored(a, aux_size, c) * depth + t * piece) // width
                pairs += [
                    ((a * blk_size + i) * occ_size + c, (a * blk_size + (i ^ away)) * occ_size + c)
                    for i in range(blk_size)
                ]
        sent = pl.pallas_call(
            functools.partial(head_kernel, piece, t),
            out_shape=jax.ShapeDtypeStruct((piece, columns), orbitals.dtype),
            in_specs=[HBM],
            out_specs=VMEM,
            scratch_shapes=[pltpu.SemaphoreType.DMA],
            compiler_params=pltpu.CompilerParams(vmem_limit_bytes=1 << 20),
            cost_estimate=cost(4 * slot_total),
            name="head",
        )(in_hbm(orbitals))
        parts.append(lax.ppermute(sent, ("aux", "blk", "occ"), pairs))
    next_block = lax.ppermute(orbitals, "blk", exchange_pairs(1, blk_size))
    chunk = parts[0] if len(parts) == 1 else jnp.concatenate(parts, 0)

    acc_shape = jax.ShapeDtypeStruct((aux_total, width, columns), jnp.float32)
    table_shape = pltpu.SMEM((2 * slot_total + 6,), jnp.int32)
    small = pltpu.CompilerParams(vmem_limit_bytes=10 << 20)
    ints = integrals

    table = pl.pallas_call(
        functools.partial(sort_kernel, depth, width),
        out_shape=table_shape,
        in_specs=[SMEM, SMEM],
        out_specs=SMEM,
        compiler_params=pltpu.CompilerParams(vmem_limit_bytes=1 << 20),
        cost_estimate=cost(1),
        name="sort",
    )(pair_counts, pair_lists)

    def near(group, coef, *acc):
        return pl.pallas_call(
            functools.partial(near_kernel, group),
            out_shape=acc_shape,
            in_specs=[SMEM, VMEM, VMEM] + [VMEM] * len(acc),
            out_specs=VMEM,
            input_output_aliases={3: 0} if acc else {},
            compiler_params=small,
            cost_estimate=cost(2),
        )(table, ints, coef, *acc)

    acc = near(0, orbitals)
    chunk, acc = lax.optimization_barrier((chunk, acc))
    chunks = [chunk] + [
        lax.ppermute(chunk, ("aux", "occ"), aux_exchange(k, aux_size, occ_size)) for k in range(1, aux_size)
    ]
    acc = near(1, next_block, acc)

    share = width // occ_size
    piece_shape = jax.ShapeDtypeStruct((width, share), jnp.float32)
    halves_shape = jax.ShapeDtypeStruct((width, aux_total * columns), jnp.bfloat16)
    far_scratch = [pltpu.VMEM((aux_size * depth, columns), jnp.bfloat16)]
    far_params = pltpu.CompilerParams(
        vmem_limit_bytes=(10 << 20) + 2 * columns * depth * aux_size
    )
    whole_pairs = (2 * depth) % width == 0
    acc = pl.pallas_call(
        functools.partial(far_kernel, (0, 1)),
        out_shape=acc_shape,
        in_specs=[SMEM] + [VMEM] * 4,
        out_specs=VMEM,
        scratch_shapes=far_scratch,
        input_output_aliases={4: 0},
        compiler_params=far_params,
        cost_estimate=cost(3),
        name="far",
    )(table, ints, *chunks[:2], acc)
    needed = tuple(range(2 if whole_pairs else 0, aux_size))
    _, halves, *pieces = pl.pallas_call(
        functools.partial(last_kernel, needed, occ_size),
        out_shape=[acc_shape, halves_shape] + [piece_shape] * (occ_size - 1),
        in_specs=[SMEM, VMEM] + [VMEM] * (aux_size + 1),
        out_specs=[VMEM] * (occ_size + 1),
        scratch_shapes=far_scratch,
        input_output_aliases={aux_size + 2: 0},
        compiler_params=far_params,
        cost_estimate=cost(3),
        name="last",
    )(table, ints, *chunks, acc)
    kept = pl.pallas_call(
        functools.partial(share_kernel, 0),
        out_shape=piece_shape,
        in_specs=[VMEM],
        out_specs=VMEM,
        compiler_params=small,
        cost_estimate=cost(1),
        name="kept",
    )(halves)

    terms = [kept] + [
        lax.ppermute(pieces[k - 1], "occ", exchange_pairs(k, occ_size)) for k in range(1, occ_size)
    ]
    rows = width // aux_size
    mine = pl.pallas_call(
        split_kernel,
        out_shape=[jax.ShapeDtypeStruct((rows, share), jnp.float32)]
        + [jax.ShapeDtypeStruct((rows + EXPONENT_ROWS, share), jnp.float32)] * (aux_size - 1),
        in_specs=[VMEM] * occ_size,
        out_specs=[VMEM] * aux_size,
        compiler_params=pltpu.CompilerParams(vmem_limit_bytes=8 << 20),
        name="split",
    )(*terms)
    total = mine[0]
    for k in range(1, aux_size):
        sent = mine[k].astype(jnp.float16)
        total = total + unscaled(lax.ppermute(sent, ("aux", "occ"), aux_exchange(k, aux_size, occ_size)), rows)
    total = total / (columns * occ_size)
    shares = [total] + [
        lax.ppermute(total, "occ", exchange_pairs(k, occ_size)) for k in range(1, occ_size)
    ]
    ordered = []
    for o in range(occ_size):
        value = shares[0]
        for k in range(1, occ_size):
            value = jnp.where((my_occ ^ k) == o, shares[k], value)
        ordered.append(value)
    return jnp.concatenate(ordered, 1)[None]


def solution(mesh):
    placed = (P("aux", "blk", None, None, None), P("blk", "occ"), P("blk", None), P("blk"))
    return jax.shard_map(
        per_device, mesh=mesh, in_specs=placed, out_specs=P("blk", "aux", None), check_vma=False
    )
```

profile of v0, /device:TPU:0, one launch (start us, length us, event | category | flops | bytes accessed | tf_op | source)
XLA Modules:
  0.0 38.6 jit_solution(2925013076728920015)
XLA Ops:
  0.0 3.1 %collective-permute-start.4 = (bf16[512,256]{1,0:T(8,128)(2,1)}, bf16[512,256]{1,0:T(8,128)(2,1)S(1)}, u32[]{:S(2)}, u32[]{:S(2)}) collective-permute-start(bf16[512,256]{1,0:T(8,128)(2,1)} %coef_ref.1), channel_id=1, source_target_pairs={{0,2},{2,0},{4,6},{6,4},{1,3},{3,1},{5,7},{7,5},{8,10},{10,8},{12,... | collective-permute-start | bytes 786440 | tf_op jit(solution)/shard_map/ppermute | solution.py:227
  3.1 1.1 %head.1 = bf16[256,256]{1,0:T(8,128)(2,1)S(1)} custom-call(bf16[512,256]{1,0:T(8,128)(2,1)} %coef_ref.1), custom_call_target="tpu_custom_call" | custom-call | flops 23622320128 | bytes 92274688 | tf_op jit(solution)/shard_map/head/pallas_call | solution.py:216
  4.1 0.0 copy-start.1
  4.1 2.7 %collective-permute-start = (bf16[256,256]{1,0:T(8,128)(2,1)S(1)}, bf16[256,256]{1,0:T(8,128)(2,1)S(1)}, u32[]{:S(2)}, u32[]{:S(2)}) collective-permute-start(bf16[256,256]{1,0:T(8,128)(2,1)S(1)} %head.1), channel_id=1, source_target_pairs={{0,4},{2,6},{4,0},{6,2},{1,5},{3,7},{5,1},{7,3},{8,12},{10,14},{12... | collective-permute-start | bytes 393224 | tf_op jit(solution)/shard_map/ppermute | solution.py:226
  8.2 0.8 %sort.1.table = s32[28]{0:T(128)S(4)} custom-call(s32[1]{0:T(128)S(6)} %copy.11.counts, s32[1,11]{1,0:T(1,128)S(1)} %copy-done.2), custom_call_target="tpu_custom_call" | custom-call | flops 536870912 | bytes 2097152 | tf_op jit(solution)/shard_map/sort/pallas_call | solution.py:235
  9.0 1.7 %copy-done = bf16[4,1,11,512,512]{4,3,2,1,0:T(8,128)(2,1)S(1)} copy-done((bf16[4,1,11,512,512]{4,3,2,1,0:T(8,128)(2,1)S(1)}, bf16[4,1,11,512,512]{4,3,2,1,0:T(8,128)(2,1)}, u32[]{:S(2)}) %copy-start) | copy-done | bytes 23068696
  10.7 0.2 copy-done.1
  10.9 1.4 %shard_map.46.accs_0_ = f32[4,512,256]{2,1,0:T(8,128)S(1)} custom-call(s32[28]{0:T(128)S(4)} %sort.1.table, bf16[4,1,11,512,512]{4,3,2,1,0:T(8,128)(2,1)S(1)} %copy-done, bf16[512,256]{1,0:T(8,128)(2,1)S(1)} %copy-done.1), custom_call_target="tpu_custom_call" | custom-call | flops 1073741824 | bytes 4194304 | tf_op jit(solution)/shard_map/pallas_call | solution.py:246
  12.3 0.0 collective-permute-done.rest_0_
  12.3 1.6 %collective-permute-start.1 = (bf16[256,256]{1,0:T(8,128)(2,1)S(1)}, bf16[256,256]{1,0:T(8,128)(2,1)S(1)}, u32[]{:S(2)}, u32[]{:S(2)}) collective-permute-start(bf16[256,256]{1,0:T(8,128)(2,1)S(1)} %collective-permute-done.rest_0_), channel_id=1, source_target_pairs={{0,8},{1,17},{8,0},{9,25},{16,24},{17,1},{24,16},{25,9},{2,10},{3,... | collective-permute-start | bytes 393224 | tf_op jit(solution)/shard_map/ppermute | solution.py:259
  13.9 3.7 %collective-permute-start.2 = (bf16[256,256]{1,0:T(8,128)(2,1)S(1)}, bf16[256,256]{1,0:T(8,128)(2,1)S(1)}, u32[]{:S(2)}, u32[]{:S(2)}) collective-permute-start(bf16[256,256]{1,0:T(8,128)(2,1)S(1)} %collective-permute-done.rest_0_), channel_id=1, source_target_pairs={{0,16},{1,9},{8,24},{9,1},{16,0},{17,25},{24,8},{25,17},{2,18},{3,... | collective-permute-start | bytes 393224 | tf_op jit(solution)/shard_map/ppermute | solution.py:259
  17.6 0.0 collective-permute-start.3
  17.6 0.0 collective-permute-done.4.coef_ref
  17.6 0.7 %shard_map.47.rest_2_ = f32[4,512,256]{2,1,0:T(8,128)S(1)} custom-call(s32[28]{0:T(128)S(4)} %sort.1.table, bf16[4,1,11,512,512]{4,3,2,1,0:T(8,128)(2,1)S(1)} %copy-done, bf16[512,256]{1,0:T(8,128)(2,1)S(1)} %collective-permute-done.4.coef_ref, f32[4,512,256]{2,1,0:T(8,128)S(1)} %shard_map.46.accs_0_), custom_call_target="tpu_custom_call", output_to_operand_aliasing={{}: (3, {})} | custom-call | flops 1073741824 | bytes 4194304 | tf_op jit(solution)/shard_map/pallas_call | solution.py:246
  18.3 0.0 collective-permute-done.1.rest_1_
  18.3 1.3 %far.1.rest_4_ = f32[4,512,256]{2,1,0:T(8,128)S(1)} custom-call(s32[28]{0:T(128)S(4)} %sort.1.table, bf16[4,1,11,512,512]{4,3,2,1,0:T(8,128)(2,1)S(1)} %copy-done, bf16[256,256]{1,0:T(8,128)(2,1)S(1)} %collective-permute-done.rest_0_, bf16[256,256]{1,0:T(8,128)(2,1)S(1)} %collective-permute-done.1.rest_1_, ...), custom_call_target="tpu_custom_call", output_to_operand_aliasing={{}: (4, {})} | custom-call | flops 1610612736 | bytes 6291456 | tf_op jit(solution)/shard_map/far/pallas_call | solution.py:271
  19.6 2.3 %collective-permute-done.2.rest_2_ = bf16[256,256]{1,0:T(8,128)(2,1)S(1)} collective-permute-done((bf16[256,256]{1,0:T(8,128)(2,1)S(1)}, bf16[256,256]{1,0:T(8,128)(2,1)S(1)}, u32[]{:S(2)}, u32[]{:S(2)}) %collective-permute-start.2) | collective-permute-done | bytes 131104 | tf_op jit(solution)/shard_map/ppermute | solution.py:259
  21.9 1.5 %collective-permute-done.3.rest_3_ = bf16[256,256]{1,0:T(8,128)(2,1)S(1)} collective-permute-done((bf16[256,256]{1,0:T(8,128)(2,1)S(1)}, bf16[256,256]{1,0:T(8,128)(2,1)S(1)}, u32[]{:S(2)}, u32[]{:S(2)}) %collective-permute-start.3) | collective-permute-done | bytes 131104 | tf_op jit(solution)/shard_map/ppermute | solution.py:259
  23.4 3.9 %last.1 = (f32[4,512,256]{2,1,0:T(8,128)S(1)}, bf16[512,1024]{1,0:T(8,128)(2,1)S(1)}, f32[512,256]{1,0:T(8,128)S(1)}) custom-call(s32[28]{0:T(128)S(4)} %sort.1.table, bf16[4,1,11,512,512]{4,3,2,1,0:T(8,128)(2,1)S(1)} %copy-done, bf16[256,256]{1,0:T(8,128)(2,1)S(1)} %collective-permute-done.rest_0_, ...), custom_call_target="tpu_custom_call", output_to_operand_aliasing={{0}: (6, {})} | custom-call | flops 1610612736 | bytes 6291456 | tf_op jit(solution)/shard_map/last/pallas_call | solution.py:283
  27.4 0.1 collective-permute-start.5
  27.4 0.5 %kept.1.refs_0_ = f32[512,256]{1,0:T(8,128)S(1)} custom-call(bf16[512,1024]{1,0:T(8,128)(2,1)S(1)} %get-tuple-element.15.halves), custom_call_target="tpu_custom_call" | custom-call | flops 536870912 | bytes 2097152 | tf_op jit(solution)/shard_map/kept/pallas_call | solution.py:294
  27.9 1.4 %collective-permute-done.5.refs_1_ = f32[512,256]{1,0:T(8,128)S(1)} collective-permute-done((f32[512,256]{1,0:T(8,128)S(1)}, f32[512,256]{1,0:T(8,128)S(1)}, u32[]{:S(2)}, u32[]{:S(2)}) %collective-permute-start.5) | collective-permute-done | bytes 524320 | tf_op jit(solution)/shard_map/ppermute | solution.py:305
  29.3 0.1 split.1
  29.4 0.8 %collective-permute-start.6 = (f16[144,256]{1,0:T(8,128)(2,1)S(1)}, f16[144,256]{1,0:T(8,128)(2,1)S(1)}, u32[]{:S(2)}, u32[]{:S(2)}) collective-permute-start(f16[144,256]{1,0:T(8,128)(2,1)S(1)} %convert_element_type.18), channel_id=1, source_target_pairs={{0,8},{1,17},{8,0},{9,25},{16,24},{17,1},{24,16},{25,9},{2,10},{3,... | collective-permute-start | bytes 221192 | tf_op jit(solution)/shard_map/ppermute | solution.py:320
  30.3 0.5 %collective-permute-start.7 = (f16[144,256]{1,0:T(8,128)(2,1)S(1)}, f16[144,256]{1,0:T(8,128)(2,1)S(1)}, u32[]{:S(2)}, u32[]{:S(2)}) collective-permute-start(f16[144,256]{1,0:T(8,128)(2,1)S(1)} %convert_element_type.20), channel_id=1, source_target_pairs={{0,16},{1,9},{8,24},{9,1},{16,0},{17,25},{24,8},{25,17},{2,18},{3,... | collective-permute-start | bytes 221192 | tf_op jit(solution)/shard_map/ppermute | solution.py:320
  30.9 2.3 %collective-permute-start.8 = (f16[144,256]{1,0:T(8,128)(2,1)S(1)}, f16[144,256]{1,0:T(8,128)(2,1)S(1)}, u32[]{:S(2)}, u32[]{:S(2)}) collective-permute-start(f16[144,256]{1,0:T(8,128)(2,1)S(1)} %convert_element_type.22), channel_id=1, source_target_pairs={{0,24},{1,25},{8,16},{9,17},{16,8},{17,9},{24,0},{25,1},{2,26},{3,... | collective-permute-start | bytes 221192 | tf_op jit(solution)/shard_map/ppermute | solution.py:320
  33.2 0.8 %collective-permute-done.6 = f16[144,256]{1,0:T(8,128)(2,1)S(1)} collective-permute-done((f16[144,256]{1,0:T(8,128)(2,1)S(1)}, f16[144,256]{1,0:T(8,128)(2,1)S(1)}, u32[]{:S(2)}, u32[]{:S(2)}) %collective-permute-start.6) | collective-permute-done | bytes 73760 | tf_op jit(solution)/shard_map/ppermute | solution.py:320
  33.9 2.3 %collective-permute-done.7 = f16[144,256]{1,0:T(8,128)(2,1)S(1)} collective-permute-done((f16[144,256]{1,0:T(8,128)(2,1)S(1)}, f16[144,256]{1,0:T(8,128)(2,1)S(1)}, u32[]{:S(2)}, u32[]{:S(2)}) %collective-permute-start.7) | collective-permute-done | bytes 73760 | tf_op jit(solution)/shard_map/ppermute | solution.py:320
  36.3 0.0 collective-permute-done.8
  36.4 0.1 collective-permute-start.9
  36.5 1.3 %collective-permute-done.9 = f32[128,256]{1,0:T(8,128)S(1)} collective-permute-done((f32[128,256]{1,0:T(8,128)S(1)}, f32[128,256]{1,0:T(8,128)S(1)}, u32[]{:S(2)}, u32[]{:S(2)}) %collective-permute-start.9) | collective-permute-done | bytes 131104 | tf_op jit(solution)/shard_map/ppermute | solution.py:323
  37.9 0.7 %maximum_bitcast_fusion = f32[1,128,512]{2,1,0:T(8,128)} fusion(f32[128,256]{1,0:T(8,128)S(1)} %get-tuple-element.22, f32[128,256]{1,0:T(8,128)S(1)} %get-tuple-element.21), kind=kLoop, calls=%fused_computation | loop fusion | flops 65536 | bytes 524288 | tf_op jit(solution)/shard_map/broadcast_in_dim | solution.py:331
  (14 shorter events, 0.2 us)
Async XLA Ops:
  0.0 8.2 %copy-start.2 = (s32[1,11]{1,0:T(1,128)S(1)}, s32[1,11]{1,0:T(1,128)}, u32[]{:S(2)}) copy-start(s32[1,11]{1,0:T(1,128)} %lists.1) | copy-start | bytes 136
  0.0 17.6 %collective-permute-start.4 = (bf16[512,256]{1,0:T(8,128)(2,1)}, bf16[512,256]{1,0:T(8,128)(2,1)S(1)}, u32[]{:S(2)}, u32[]{:S(2)}) collective-permute-start(bf16[512,256]{1,0:T(8,128)(2,1)} %coef_ref.1), channel_id=1, source_target_pairs={{0,2},{2,0},{4,6},{6,4},{1,3},{3,1},{5,7},{7,5},{8,10},{10,8},{12,... | collective-permute-start | bytes 786440 | tf_op jit(solution)/shard_map/ppermute | solution.py:227
  3.1 7.6 %copy-start = (bf16[4,1,11,512,512]{4,3,2,1,0:T(8,128)(2,1)S(1)}, bf16[4,1,11,512,512]{4,3,2,1,0:T(8,128)(2,1)}, u32[]{:S(2)}) copy-start(bf16[4,1,11,512,512]{4,3,2,1,0:T(8,128)(2,1)} %ints_ref.7) | copy-start | bytes 69206016
  4.1 6.7 %copy-start.1 = (bf16[512,256]{1,0:T(8,128)(2,1)S(1)}, bf16[512,256]{1,0:T(8,128)(2,1)}, u32[]{:S(2)}) copy-start(bf16[512,256]{1,0:T(8,128)(2,1)} %coef_ref.1) | copy-start | bytes 786436
  4.1 8.1 %collective-permute-start = (bf16[256,256]{1,0:T(8,128)(2,1)S(1)}, bf16[256,256]{1,0:T(8,128)(2,1)S(1)}, u32[]{:S(2)}, u32[]{:S(2)}) collective-permute-start(bf16[256,256]{1,0:T(8,128)(2,1)S(1)} %head.1), channel_id=1, source_target_pairs={{0,4},{2,6},{4,0},{6,2},{1,5},{3,7},{5,1},{7,3},{8,12},{10,14},{12... | collective-permute-start | bytes 393224 | tf_op jit(solution)/shard_map/ppermute | solution.py:226
  12.3 6.0 %collective-permute-start.1 = (bf16[256,256]{1,0:T(8,128)(2,1)S(1)}, bf16[256,256]{1,0:T(8,128)(2,1)S(1)}, u32[]{:S(2)}, u32[]{:S(2)}) collective-permute-start(bf16[256,256]{1,0:T(8,128)(2,1)S(1)} %collective-permute-done.rest_0_), channel_id=1, source_target_pairs={{0,8},{1,17},{8,0},{9,25},{16,24},{17,1},{24,16},{25,9},{2,10},{3,... | collective-permute-start | bytes 393224 | tf_op jit(solution)/shard_map/ppermute | solution.py:259
  13.9 8.1 %collective-permute-start.2 = (bf16[256,256]{1,0:T(8,128)(2,1)S(1)}, bf16[256,256]{1,0:T(8,128)(2,1)S(1)}, u32[]{:S(2)}, u32[]{:S(2)}) collective-permute-start(bf16[256,256]{1,0:T(8,128)(2,1)S(1)} %collective-permute-done.rest_0_), channel_id=1, source_target_pairs={{0,16},{1,9},{8,24},{9,1},{16,0},{17,25},{24,8},{25,17},{2,18},{3,... | collective-permute-start | bytes 393224 | tf_op jit(solution)/shard_map/ppermute | solution.py:259
  17.6 5.9 %collective-permute-start.3 = (bf16[256,256]{1,0:T(8,128)(2,1)S(1)}, bf16[256,256]{1,0:T(8,128)(2,1)S(1)}, u32[]{:S(2)}, u32[]{:S(2)}) collective-permute-start(bf16[256,256]{1,0:T(8,128)(2,1)S(1)} %collective-permute-done.rest_0_), channel_id=1, source_target_pairs={{0,24},{1,25},{8,16},{9,17},{16,8},{17,9},{24,0},{25,1},{2,26},{3,... | collective-permute-start | bytes 393224 | tf_op jit(solution)/shard_map/ppermute | solution.py:259
  27.4 2.0 %collective-permute-start.5 = (f32[512,256]{1,0:T(8,128)S(1)}, f32[512,256]{1,0:T(8,128)S(1)}, u32[]{:S(2)}, u32[]{:S(2)}) collective-permute-start(f32[512,256]{1,0:T(8,128)S(1)} %get-tuple-element.16), channel_id=1, source_target_pairs={{0,1},{1,0},{2,3},{3,2},{4,5},{5,4},{6,7},{7,6},{8,9},{9,8},{10,11... | collective-permute-start | bytes 1572872 | tf_op jit(solution)/shard_map/ppermute | solution.py:305
  29.4 4.5 %collective-permute-start.6 = (f16[144,256]{1,0:T(8,128)(2,1)S(1)}, f16[144,256]{1,0:T(8,128)(2,1)S(1)}, u32[]{:S(2)}, u32[]{:S(2)}) collective-permute-start(f16[144,256]{1,0:T(8,128)(2,1)S(1)} %convert_element_type.18), channel_id=1, source_target_pairs={{0,8},{1,17},{8,0},{9,25},{16,24},{17,1},{24,16},{25,9},{2,10},{3,... | collective-permute-start | bytes 221192 | tf_op jit(solution)/shard_map/ppermute | solution.py:320
  30.3 6.0 %collective-permute-start.7 = (f16[144,256]{1,0:T(8,128)(2,1)S(1)}, f16[144,256]{1,0:T(8,128)(2,1)S(1)}, u32[]{:S(2)}, u32[]{:S(2)}) collective-permute-start(f16[144,256]{1,0:T(8,128)(2,1)S(1)} %convert_element_type.20), channel_id=1, source_target_pairs={{0,16},{1,9},{8,24},{9,1},{16,0},{17,25},{24,8},{25,17},{2,18},{3,... | collective-permute-start | bytes 221192 | tf_op jit(solution)/shard_map/ppermute | solution.py:320
  30.9 5.5 %collective-permute-start.8 = (f16[144,256]{1,0:T(8,128)(2,1)S(1)}, f16[144,256]{1,0:T(8,128)(2,1)S(1)}, u32[]{:S(2)}, u32[]{:S(2)}) collective-permute-start(f16[144,256]{1,0:T(8,128)(2,1)S(1)} %convert_element_type.22), channel_id=1, source_target_pairs={{0,24},{1,25},{8,16},{9,17},{16,8},{17,9},{24,0},{25,1},{2,26},{3,... | collective-permute-start | bytes 221192 | tf_op jit(solution)/shard_map/ppermute | solution.py:320
  36.4 1.4 %collective-permute-start.9 = (f32[128,256]{1,0:T(8,128)S(1)}, f32[128,256]{1,0:T(8,128)S(1)}, u32[]{:S(2)}, u32[]{:S(2)}) collective-permute-start(f32[128,256]{1,0:T(8,128)S(1)} %fusion.1), channel_id=1, source_target_pairs={{0,1},{1,0},{2,3},{3,2},{4,5},{5,4},{6,7},{7,6},{8,9},{9,8},{10,11... | collective-permute-start | bytes 393224 | tf_op jit(solution)/shard_map/ppermute | solution.py:323
where the time goes:
time: 38.7 us; the launch traced here: 38.6 us
  starting transfers between devices  14.8 us (38%)
  Pallas kernels  9.71 us (25%)
  waiting for transfers between devices  9.68 us (25%)
  local copies, waits for them, and re-layouts  1.85 us (5%)
  between operations  1.63 us (4%)
  other arithmetic  0.89 us (2%)
    ppermute x3, starting transfers between devices, per_device(): lax.ppermute(chunk, ('aux', 'occ'), aux_exchange(k, aux_size, occ_size))  5.29 us
    pallas_call x1, Pallas kernels, per_device(): pl.pallas_call(functools.partial(last_kernel, needed, occ_size), out_shap...  3.89 us
    ppermute x3, waiting for transfers between devices, per_device(): lax.ppermute(chunk, ('aux', 'occ'), aux_exchange(k, aux_size, occ_size))  3.83 us
    ppermute x3, starting transfers between devices, per_device(): lax.ppermute(sent, ('aux', 'occ'), aux_exchange(k, aux_size, occ_size))  3.68 us
    ppermute x3, waiting for transfers between devices, per_device(): lax.ppermute(sent, ('aux', 'occ'), aux_exchange(k, aux_size, occ_size))  3.1 us
    ppermute x1, starting transfers between devices, per_device(): next_block = lax.ppermute(orbitals, 'blk', exchange_pairs(1, blk_size))  3.05 us
    ppermute x1, starting transfers between devices, per_device(): parts.append(lax.ppermute(sent, ('aux', 'blk', 'occ'), pairs))  2.65 us
    pallas_call x2, Pallas kernels, near(): pl.pallas_call(functools.partial(near_kernel, group), out_shape=acc_shape...  2.12 us
  transfers between devices with their start and end apart: 10, of which 6 were waited for; matrix products, arithmetic and copies ran while one was open for 0% of the time, Pallas kernels for 15%

commit v1 on v0

--- a/solution.py
+++ b/solution.py
@@ -166,11 +166,10 @@
 def split_kernel(*refs):
     aux_size, occ_size = lax.axis_size("aux"), lax.axis_size("occ")
     terms, outs = refs[:occ_size], refs[occ_size:]
-    my_aux, my_occ = lax.axis_index("aux"), lax.axis_index("occ")
+    my_aux = lax.axis_index("aux")
     depth = outs[0].shape[0]
     for k in range(aux_size):
-        target = my_aux ^ mirrored(k, aux_size, my_occ)
-        rows = pl.ds(pl.multiple_of(target * depth, depth), depth)
+        rows = pl.ds(pl.multiple_of((my_aux ^ k) * depth, depth), depth)
         total = terms[0][rows, :]
         for term in terms[1:]:
             total = total + term[rows, :]
@@ -317,7 +316,7 @@
     total = mine[0]
     for k in range(1, aux_size):
         sent = mine[k].astype(jnp.float16)
-        total = total + unscaled(lax.ppermute(sent, ("aux", "occ"), aux_exchange(k, aux_size, occ_size)), rows)
+        total = total + unscaled(lax.ppermute(sent, "aux", exchange_pairs(k, aux_size)), rows)
     total = total / (columns * occ_size)
     shares = [total] + [
         lax.ppermute(total, "occ", exchange_pairs(k, occ_size)) for k in range(1, occ_size)

time: 38.7 us -> 38.7 us (level)
  no operation moved by 1% of the time
where the time goes in v1:
time: 38.7 us; the launch traced here: 38.6 us
  starting transfers between devices  14.8 us (38%)
  Pallas kernels  9.71 us (25%)
  waiting for transfers between devices  9.68 us (25%)
  local copies, waits for them, and re-layouts  1.85 us (5%)
  between operations  1.63 us (4%)
  other arithmetic  0.89 us (2%)
    ppermute x3, starting transfers between devices, per_device(): lax.ppermute(chunk, ('aux', 'occ'), aux_exchange(k, aux_size, occ_size))  5.29 us
    pallas_call x1, Pallas kernels, per_device(): pl.pallas_call(functools.partial(last_kernel, needed, occ_size), out_shap...  3.89 us
    ppermute x3, waiting for transfers between devices, per_device(): lax.ppermute(chunk, ('aux', 'occ'), aux_exchange(k, aux_size, occ_size))  3.83 us
    ppermute x3, starting transfers between devices, per_device(): lax.ppermute(sent, 'aux', exchange_pairs(k, aux_size))  3.68 us
    ppermute x3, waiting for transfers between devices, per_device(): lax.ppermute(sent, 'aux', exchange_pairs(k, aux_size))  3.1 us
    ppermute x1, starting transfers between devices, per_device(): next_block = lax.ppermute(orbitals, 'blk', exchange_pairs(1, blk_size))  3.05 us
    ppermute x1, starting transfers between devices, per_device(): parts.append(lax.ppermute(sent, ('aux', 'blk', 'occ'), pairs))  2.65 us
    pallas_call x2, Pallas kernels, near(): pl.pallas_call(functools.partial(near_kernel, group), out_shape=acc_shape...  2.12 us
  transfers between devices with their start and end apart: 10, of which 6 were waited for; matrix products, arithmetic and copies ran while one was open for 0% of the time, Pallas kernels for 15%

profile of v1, /device:TPU:0, one launch (start us, length us, event | category | flops | bytes accessed | tf_op | source)
XLA Modules:
  0.0 38.6 jit_solution(14847160571003780394)
XLA Ops:
  0.0 3.1 %collective-permute-start.4 = (bf16[512,256]{1,0:T(8,128)(2,1)}, bf16[512,256]{1,0:T(8,128)(2,1)S(1)}, u32[]{:S(2)}, u32[]{:S(2)}) collective-permute-start(bf16[512,256]{1,0:T(8,128)(2,1)} %coef_ref.1), channel_id=1, source_target_pairs={{0,2},{2,0},{4,6},{6,4},{1,3},{3,1},{5,7},{7,5},{8,10},{10,8},{12,... | collective-permute-start | bytes 786440 | tf_op jit(solution)/shard_map/ppermute | solution.py:226
  3.1 1.1 %head.1 = bf16[256,256]{1,0:T(8,128)(2,1)S(1)} custom-call(bf16[512,256]{1,0:T(8,128)(2,1)} %coef_ref.1), custom_call_target="tpu_custom_call" | custom-call | flops 23622320128 | bytes 92274688 | tf_op jit(solution)/shard_map/head/pallas_call | solution.py:215
  4.1 0.0 copy-start.1
  4.1 2.7 %collective-permute-start = (bf16[256,256]{1,0:T(8,128)(2,1)S(1)}, bf16[256,256]{1,0:T(8,128)(2,1)S(1)}, u32[]{:S(2)}, u32[]{:S(2)}) collective-permute-start(bf16[256,256]{1,0:T(8,128)(2,1)S(1)} %head.1), channel_id=1, source_target_pairs={{0,4},{2,6},{4,0},{6,2},{1,5},{3,7},{5,1},{7,3},{8,12},{10,14},{12... | collective-permute-start | bytes 393224 | tf_op jit(solution)/shard_map/ppermute | solution.py:225
  8.2 0.8 %sort.1.table = s32[28]{0:T(128)S(4)} custom-call(s32[1]{0:T(128)S(6)} %copy.11.counts, s32[1,11]{1,0:T(1,128)S(1)} %copy-done.2), custom_call_target="tpu_custom_call" | custom-call | flops 536870912 | bytes 2097152 | tf_op jit(solution)/shard_map/sort/pallas_call | solution.py:234
  9.0 1.7 %copy-done = bf16[4,1,11,512,512]{4,3,2,1,0:T(8,128)(2,1)S(1)} copy-done((bf16[4,1,11,512,512]{4,3,2,1,0:T(8,128)(2,1)S(1)}, bf16[4,1,11,512,512]{4,3,2,1,0:T(8,128)(2,1)}, u32[]{:S(2)}) %copy-start) | copy-done | bytes 23068696
  10.7 0.2 copy-done.1
  10.9 1.4 %shard_map.46.accs_0_ = f32[4,512,256]{2,1,0:T(8,128)S(1)} custom-call(s32[28]{0:T(128)S(4)} %sort.1.table, bf16[4,1,11,512,512]{4,3,2,1,0:T(8,128)(2,1)S(1)} %copy-done, bf16[512,256]{1,0:T(8,128)(2,1)S(1)} %copy-done.1), custom_call_target="tpu_custom_call" | custom-call | flops 1073741824 | bytes 4194304 | tf_op jit(solution)/shard_map/pallas_call | solution.py:245
  12.3 0.0 collective-permute-done.rest_0_
  12.3 1.6 %collective-permute-start.1 = (bf16[256,256]{1,0:T(8,128)(2,1)S(1)}, bf16[256,256]{1,0:T(8,128)(2,1)S(1)}, u32[]{:S(2)}, u32[]{:S(2)}) collective-permute-start(bf16[256,256]{1,0:T(8,128)(2,1)S(1)} %collective-permute-done.rest_0_), channel_id=1, source_target_pairs={{0,8},{1,17},{8,0},{9,25},{16,24},{17,1},{24,16},{25,9},{2,10},{3,... | collective-permute-start | bytes 393224 | tf_op jit(solution)/shard_map/ppermute | solution.py:258
  13.9 3.7 %collective-permute-start.2 = (bf16[256,256]{1,0:T(8,128)(2,1)S(1)}, bf16[256,256]{1,0:T(8,128)(2,1)S(1)}, u32[]{:S(2)}, u32[]{:S(2)}) collective-permute-start(bf16[256,256]{1,0:T(8,128)(2,1)S(1)} %collective-permute-done.rest_0_), channel_id=1, source_target_pairs={{0,16},{1,9},{8,24},{9,1},{16,0},{17,25},{24,8},{25,17},{2,18},{3,... | collective-permute-start | bytes 393224 | tf_op jit(solution)/shard_map/ppermute | solution.py:258
  17.6 0.0 collective-permute-start.3
  17.6 0.0 collective-permute-done.4.coef_ref
  17.6 0.7 %shard_map.47.rest_2_ = f32[4,512,256]{2,1,0:T(8,128)S(1)} custom-call(s32[28]{0:T(128)S(4)} %sort.1.table, bf16[4,1,11,512,512]{4,3,2,1,0:T(8,128)(2,1)S(1)} %copy-done, bf16[512,256]{1,0:T(8,128)(2,1)S(1)} %collective-permute-done.4.coef_ref, f32[4,512,256]{2,1,0:T(8,128)S(1)} %shard_map.46.accs_0_), custom_call_target="tpu_custom_call", output_to_operand_aliasing={{}: (3, {})} | custom-call | flops 1073741824 | bytes 4194304 | tf_op jit(solution)/shard_map/pallas_call | solution.py:245
  18.3 0.0 collective-permute-done.1.rest_1_
  18.3 1.3 %far.1.rest_4_ = f32[4,512,256]{2,1,0:T(8,128)S(1)} custom-call(s32[28]{0:T(128)S(4)} %sort.1.table, bf16[4,1,11,512,512]{4,3,2,1,0:T(8,128)(2,1)S(1)} %copy-done, bf16[256,256]{1,0:T(8,128)(2,1)S(1)} %collective-permute-done.rest_0_, bf16[256,256]{1,0:T(8,128)(2,1)S(1)} %collective-permute-done.1.rest_1_, ...), custom_call_target="tpu_custom_call", output_to_operand_aliasing={{}: (4, {})} | custom-call | flops 1610612736 | bytes 6291456 | tf_op jit(solution)/shard_map/far/pallas_call | solution.py:270
  19.6 2.3 %collective-permute-done.2.rest_2_ = bf16[256,256]{1,0:T(8,128)(2,1)S(1)} collective-permute-done((bf16[256,256]{1,0:T(8,128)(2,1)S(1)}, bf16[256,256]{1,0:T(8,128)(2,1)S(1)}, u32[]{:S(2)}, u32[]{:S(2)}) %collective-permute-start.2) | collective-permute-done | bytes 131104 | tf_op jit(solution)/shard_map/ppermute | solution.py:258
  21.9 1.5 %collective-permute-done.3.rest_3_ = bf16[256,256]{1,0:T(8,128)(2,1)S(1)} collective-permute-done((bf16[256,256]{1,0:T(8,128)(2,1)S(1)}, bf16[256,256]{1,0:T(8,128)(2,1)S(1)}, u32[]{:S(2)}, u32[]{:S(2)}) %collective-permute-start.3) | collective-permute-done | bytes 131104 | tf_op jit(solution)/shard_map/ppermute | solution.py:258
  23.4 3.9 %last.1 = (f32[4,512,256]{2,1,0:T(8,128)S(1)}, bf16[512,1024]{1,0:T(8,128)(2,1)S(1)}, f32[512,256]{1,0:T(8,128)S(1)}) custom-call(s32[28]{0:T(128)S(4)} %sort.1.table, bf16[4,1,11,512,512]{4,3,2,1,0:T(8,128)(2,1)S(1)} %copy-done, bf16[256,256]{1,0:T(8,128)(2,1)S(1)} %collective-permute-done.rest_0_, ...), custom_call_target="tpu_custom_call", output_to_operand_aliasing={{0}: (6, {})} | custom-call | flops 1610612736 | bytes 6291456 | tf_op jit(solution)/shard_map/last/pallas_call | solution.py:282
  27.4 0.1 collective-permute-start.5
  27.4 0.5 %kept.1.refs_0_ = f32[512,256]{1,0:T(8,128)S(1)} custom-call(bf16[512,1024]{1,0:T(8,128)(2,1)S(1)} %get-tuple-element.15.halves), custom_call_target="tpu_custom_call" | custom-call | flops 536870912 | bytes 2097152 | tf_op jit(solution)/shard_map/kept/pallas_call | solution.py:293
  27.9 1.4 %collective-permute-done.5.refs_1_ = f32[512,256]{1,0:T(8,128)S(1)} collective-permute-done((f32[512,256]{1,0:T(8,128)S(1)}, f32[512,256]{1,0:T(8,128)S(1)}, u32[]{:S(2)}, u32[]{:S(2)}) %collective-permute-start.5) | collective-permute-done | bytes 524320 | tf_op jit(solution)/shard_map/ppermute | solution.py:304
  29.3 0.1 split.1
  29.4 0.8 %collective-permute-start.6 = (f16[144,256]{1,0:T(8,128)(2,1)S(1)}, f16[144,256]{1,0:T(8,128)(2,1)S(1)}, u32[]{:S(2)}, u32[]{:S(2)}) collective-permute-start(f16[144,256]{1,0:T(8,128)(2,1)S(1)} %convert_element_type.18), channel_id=1, source_target_pairs={{0,8},{8,0},{16,24},{24,16},{1,9},{9,1},{17,25},{25,17},{2,10},{10... | collective-permute-start | bytes 221192 | tf_op jit(solution)/shard_map/ppermute | solution.py:319
  30.3 0.5 %collective-permute-start.7 = (f16[144,256]{1,0:T(8,128)(2,1)S(1)}, f16[144,256]{1,0:T(8,128)(2,1)S(1)}, u32[]{:S(2)}, u32[]{:S(2)}) collective-permute-start(f16[144,256]{1,0:T(8,128)(2,1)S(1)} %convert_element_type.20), channel_id=1, source_target_pairs={{0,16},{8,24},{16,0},{24,8},{1,17},{9,25},{17,1},{25,9},{2,18},{10... | collective-permute-start | bytes 221192 | tf_op jit(solution)/shard_map/ppermute | solution.py:319
  30.9 2.3 %collective-permute-start.8 = (f16[144,256]{1,0:T(8,128)(2,1)S(1)}, f16[144,256]{1,0:T(8,128)(2,1)S(1)}, u32[]{:S(2)}, u32[]{:S(2)}) collective-permute-start(f16[144,256]{1,0:T(8,128)(2,1)S(1)} %convert_element_type.22), channel_id=1, source_target_pairs={{0,24},{8,16},{16,8},{24,0},{1,25},{9,17},{17,9},{25,1},{2,26},{10... | collective-permute-start | bytes 221192 | tf_op jit(solution)/shard_map/ppermute | solution.py:319
  33.2 0.7 %collective-permute-done.6 = f16[144,256]{1,0:T(8,128)(2,1)S(1)} collective-permute-done((f16[144,256]{1,0:T(8,128)(2,1)S(1)}, f16[144,256]{1,0:T(8,128)(2,1)S(1)}, u32[]{:S(2)}, u32[]{:S(2)}) %collective-permute-start.6) | collective-permute-done | bytes 73760 | tf_op jit(solution)/shard_map/ppermute | solution.py:319
  33.9 2.4 %collective-permute-done.7 = f16[144,256]{1,0:T(8,128)(2,1)S(1)} collective-permute-done((f16[144,256]{1,0:T(8,128)(2,1)S(1)}, f16[144,256]{1,0:T(8,128)(2,1)S(1)}, u32[]{:S(2)}, u32[]{:S(2)}) %collective-permute-start.7) | collective-permute-done | bytes 73760 | tf_op jit(solution)/shard_map/ppermute | solution.py:319
  36.3 0.0 collective-permute-done.8
  36.4 0.1 collective-permute-start.9
  36.5 1.3 %collective-permute-done.9 = f32[128,256]{1,0:T(8,128)S(1)} collective-permute-done((f32[128,256]{1,0:T(8,128)S(1)}, f32[128,256]{1,0:T(8,128)S(1)}, u32[]{:S(2)}, u32[]{:S(2)}) %collective-permute-start.9) | collective-permute-done | bytes 131104 | tf_op jit(solution)/shard_map/ppermute | solution.py:322
  37.9 0.7 %maximum_bitcast_fusion = f32[1,128,512]{2,1,0:T(8,128)} fusion(f32[128,256]{1,0:T(8,128)S(1)} %get-tuple-element.22, f32[128,256]{1,0:T(8,128)S(1)} %get-tuple-element.21), kind=kLoop, calls=%fused_computation | loop fusion | flops 65536 | bytes 524288 | tf_op jit(solution)/shard_map/broadcast_in_dim | solution.py:330
  (14 shorter events, 0.2 us)
Async XLA Ops:
  0.0 8.2 %copy-start.2 = (s32[1,11]{1,0:T(1,128)S(1)}, s32[1,11]{1,0:T(1,128)}, u32[]{:S(2)}) copy-start(s32[1,11]{1,0:T(1,128)} %lists.1) | copy-start | bytes 136
  0.0 17.6 %collective-permute-start.4 = (bf16[512,256]{1,0:T(8,128)(2,1)}, bf16[512,256]{1,0:T(8,128)(2,1)S(1)}, u32[]{:S(2)}, u32[]{:S(2)}) collective-permute-start(bf16[512,256]{1,0:T(8,128)(2,1)} %coef_ref.1), channel_id=1, source_target_pairs={{0,2},{2,0},{4,6},{6,4},{1,3},{3,1},{5,7},{7,5},{8,10},{10,8},{12,... | collective-permute-start | bytes 786440 | tf_op jit(solution)/shard_map/ppermute | solution.py:226
  3.1 7.6 %copy-start = (bf16[4,1,11,512,512]{4,3,2,1,0:T(8,128)(2,1)S(1)}, bf16[4,1,11,512,512]{4,3,2,1,0:T(8,128)(2,1)}, u32[]{:S(2)}) copy-start(bf16[4,1,11,512,512]{4,3,2,1,0:T(8,128)(2,1)} %ints_ref.7) | copy-start | bytes 69206016
  4.1 6.7 %copy-start.1 = (bf16[512,256]{1,0:T(8,128)(2,1)S(1)}, bf16[512,256]{1,0:T(8,128)(2,1)}, u32[]{:S(2)}) copy-start(bf16[512,256]{1,0:T(8,128)(2,1)} %coef_ref.1) | copy-start | bytes 786436
  4.1 8.1 %collective-permute-start = (bf16[256,256]{1,0:T(8,128)(2,1)S(1)}, bf16[256,256]{1,0:T(8,128)(2,1)S(1)}, u32[]{:S(2)}, u32[]{:S(2)}) collective-permute-start(bf16[256,256]{1,0:T(8,128)(2,1)S(1)} %head.1), channel_id=1, source_target_pairs={{0,4},{2,6},{4,0},{6,2},{1,5},{3,7},{5,1},{7,3},{8,12},{10,14},{12... | collective-permute-start | bytes 393224 | tf_op jit(solution)/shard_map/ppermute | solution.py:225
  12.3 6.0 %collective-permute-start.1 = (bf16[256,256]{1,0:T(8,128)(2,1)S(1)}, bf16[256,256]{1,0:T(8,128)(2,1)S(1)}, u32[]{:S(2)}, u32[]{:S(2)}) collective-permute-start(bf16[256,256]{1,0:T(8,128)(2,1)S(1)} %collective-permute-done.rest_0_), channel_id=1, source_target_pairs={{0,8},{1,17},{8,0},{9,25},{16,24},{17,1},{24,16},{25,9},{2,10},{3,... | collective-permute-start | bytes 393224 | tf_op jit(solution)/shard_map/ppermute | solution.py:258
  13.9 8.1 %collective-permute-start.2 = (bf16[256,256]{1,0:T(8,128)(2,1)S(1)}, bf16[256,256]{1,0:T(8,128)(2,1)S(1)}, u32[]{:S(2)}, u32[]{:S(2)}) collective-permute-start(bf16[256,256]{1,0:T(8,128)(2,1)S(1)} %collective-permute-done.rest_0_), channel_id=1, source_target_pairs={{0,16},{1,9},{8,24},{9,1},{16,0},{17,25},{24,8},{25,17},{2,18},{3,... | collective-permute-start | bytes 393224 | tf_op jit(solution)/shard_map/ppermute | solution.py:258
  17.6 5.9 %collective-permute-start.3 = (bf16[256,256]{1,0:T(8,128)(2,1)S(1)}, bf16[256,256]{1,0:T(8,128)(2,1)S(1)}, u32[]{:S(2)}, u32[]{:S(2)}) collective-permute-start(bf16[256,256]{1,0:T(8,128)(2,1)S(1)} %collective-permute-done.rest_0_), channel_id=1, source_target_pairs={{0,24},{1,25},{8,16},{9,17},{16,8},{17,9},{24,0},{25,1},{2,26},{3,... | collective-permute-start | bytes 393224 | tf_op jit(solution)/shard_map/ppermute | solution.py:258
  27.4 2.0 %collective-permute-start.5 = (f32[512,256]{1,0:T(8,128)S(1)}, f32[512,256]{1,0:T(8,128)S(1)}, u32[]{:S(2)}, u32[]{:S(2)}) collective-permute-start(f32[512,256]{1,0:T(8,128)S(1)} %get-tuple-element.16), channel_id=1, source_target_pairs={{0,1},{1,0},{2,3},{3,2},{4,5},{5,4},{6,7},{7,6},{8,9},{9,8},{10,11... | collective-permute-start | bytes 1572872 | tf_op jit(solution)/shard_map/ppermute | solution.py:304
  29.4 4.4 %collective-permute-start.6 = (f16[144,256]{1,0:T(8,128)(2,1)S(1)}, f16[144,256]{1,0:T(8,128)(2,1)S(1)}, u32[]{:S(2)}, u32[]{:S(2)}) collective-permute-start(f16[144,256]{1,0:T(8,128)(2,1)S(1)} %convert_element_type.18), channel_id=1, source_target_pairs={{0,8},{8,0},{16,24},{24,16},{1,9},{9,1},{17,25},{25,17},{2,10},{10... | collective-permute-start | bytes 221192 | tf_op jit(solution)/shard_map/ppermute | solution.py:319
  30.3 6.0 %collective-permute-start.7 = (f16[144,256]{1,0:T(8,128)(2,1)S(1)}, f16[144,256]{1,0:T(8,128)(2,1)S(1)}, u32[]{:S(2)}, u32[]{:S(2)}) collective-permute-start(f16[144,256]{1,0:T(8,128)(2,1)S(1)} %convert_element_type.20), channel_id=1, source_target_pairs={{0,16},{8,24},{16,0},{24,8},{1,17},{9,25},{17,1},{25,9},{2,18},{10... | collective-permute-start | bytes 221192 | tf_op jit(solution)/shard_map/ppermute | solution.py:319
  30.9 5.5 %collective-permute-start.8 = (f16[144,256]{1,0:T(8,128)(2,1)S(1)}, f16[144,256]{1,0:T(8,128)(2,1)S(1)}, u32[]{:S(2)}, u32[]{:S(2)}) collective-permute-start(f16[144,256]{1,0:T(8,128)(2,1)S(1)} %convert_element_type.22), channel_id=1, source_target_pairs={{0,24},{8,16},{16,8},{24,0},{1,25},{9,17},{17,9},{25,1},{2,26},{10... | collective-permute-start | bytes 221192 | tf_op jit(solution)/shard_map/ppermute | solution.py:319
  36.4 1.4 %collective-permute-start.9 = (f32[128,256]{1,0:T(8,128)S(1)}, f32[128,256]{1,0:T(8,128)S(1)}, u32[]{:S(2)}, u32[]{:S(2)}) collective-permute-start(f32[128,256]{1,0:T(8,128)S(1)} %fusion.1), channel_id=1, source_target_pairs={{0,1},{1,0},{2,3},{3,2},{4,5},{5,4},{6,7},{7,6},{8,9},{9,8},{10,11... | collective-permute-start | bytes 393224 | tf_op jit(solution)/shard_map/ppermute | solution.py:322

commit v2 on v1

--- a/solution.py
+++ b/solution.py
@@ -53,6 +53,10 @@
         block.reshape(aux_total * width, width), coef, preferred_element_type=jnp.float32
     )
     return product.reshape(aux_total, width, coef.shape[1])
+
+
+GROUPS = 5
+OWN_FIRST = 3
 
 
 def add_slots(table, group, ints_ref, coef_rows, acc_ref, fresh=False):
@@ -96,14 +100,15 @@
     me, seat = lax.axis_index("blk"), my_seat()
     live = counts[0]
     piece = math.gcd(far_depth, width)
-    groups, sizes = [], [jnp.int32(0)] * 4
+    groups, sizes = [], [jnp.int32(0)] * GROUPS
     for slot in range(slot_total):
         away = lists[0, slot] ^ me
         last = jnp.int32(0)
         for part in range(width // piece):
             last = jnp.maximum(last, lax.div((away - 2) * width + part * piece, far_depth) ^ seat)
-        far_group = jnp.where(last <= 1, 2, 3)
-        groups.append(jnp.where(slot < live, jnp.where(away < 2, away, far_group), 4))
+        own_group = jnp.where(sizes[0] < OWN_FIRST, 0, 1)
+        group = jnp.where(away < 2, jnp.where(away == 0, own_group, 2), jnp.where(last <= 1, 3, 4))
+        groups.append(jnp.where(slot < live, group, GROUPS))
         sizes = [n + (groups[-1] == g).astype(jnp.int32) for g, n in enumerate(sizes)]
     cursors, found = [], jnp.int32(0)
     for group, size in enumerate(sizes):
@@ -112,15 +117,17 @@
         table[2 * slot_total + 2 + group] = found
     for slot in range(slot_total):
         place = jnp.int32(slot_total)
-        for group in range(4):
+        for group in range(GROUPS):
             place = jnp.where(groups[slot] == group, cursors[group], place)
         cursors = [n + (groups[slot] == g).astype(jnp.int32) for g, n in enumerate(cursors)]
         table[place] = slot
         table[slot_total + 1 + place] = lists[0, slot] ^ me
 
 
-def near_kernel(group, table, ints_ref, coef_ref, *accs):
-    add_slots(table, group, ints_ref, lambda i: coef_ref[...], accs[-1], fresh=group == 0)
+def near_kernel(groups, table, ints_ref, *rest):
+    coefs, acc_ref = rest[: len(groups)], rest[-1]
+    for group, coef_ref in zip(groups, coefs):
+        add_slots(table, group, ints_ref, lambda i: coef_ref[...], acc_ref, fresh=group == 0)
 
 
 def add_far(group, needed, table, ints_ref, chunks, coef, acc_ref):
@@ -140,13 +147,13 @@
 
 def far_kernel(needed, table, ints_ref, *rest):
     *chunks, _, acc_ref, coef = rest
-    add_far(2, needed, table, ints_ref, chunks, coef, acc_ref)
+    add_far(3, needed, table, ints_ref, chunks, coef, acc_ref)
 
 
 def last_kernel(needed, occ_size, table, ints_ref, *rest):
     *chunks, _, acc_ref, halves = rest[: -occ_size]
     pieces, coef = rest[-occ_size:-1], rest[-1]
-    add_far(3, needed, table, ints_ref, chunks, coef, acc_ref)
+    add_far(4, needed, table, ints_ref, chunks, coef, acc_ref)
     columns = acc_ref.shape[2]
     for p in range(acc_ref.shape[0]):
         halves[:, p * columns : (p + 1) * columns] = acc_ref[p].astype(jnp.bfloat16)
@@ -227,7 +234,7 @@
     chunk = parts[0] if len(parts) == 1 else jnp.concatenate(parts, 0)
 
     acc_shape = jax.ShapeDtypeStruct((aux_total, width, columns), jnp.float32)
-    table_shape = pltpu.SMEM((2 * slot_total + 6,), jnp.int32)
+    table_shape = pltpu.SMEM((2 * slot_total + 2 + GROUPS,), jnp.int32)
     small = pltpu.CompilerParams(vmem_limit_bytes=10 << 20)
     ints = integrals
 
@@ -241,23 +248,23 @@
         name="sort",
     )(pair_counts, pair_lists)
 
-    def near(group, coef, *acc):
+    def near(groups, coefs, *acc):
         return pl.pallas_call(
-            functools.partial(near_kernel, group),
+            functools.partial(near_kernel, groups),
             out_shape=acc_shape,
-            in_specs=[SMEM, VMEM, VMEM] + [VMEM] * len(acc),
+            in_specs=[SMEM, VMEM] + [VMEM] * (len(coefs) + len(acc)),
             out_specs=VMEM,
-            input_output_aliases={3: 0} if acc else {},
+            input_output_aliases={2 + len(coefs): 0} if acc else {},
             compiler_params=small,
             cost_estimate=cost(2),
-        )(table, ints, coef, *acc)
-
-    acc = near(0, orbitals)
+        )(table, ints, *coefs, *acc)
+
+    acc = near((0,), (orbitals,))
     chunk, acc = lax.optimization_barrier((chunk, acc))
     chunks = [chunk] + [
         lax.ppermute(chunk, ("aux", "occ"), aux_exchange(k, aux_size, occ_size)) for k in range(1, aux_size)
     ]
-    acc = near(1, next_block, acc)
+    acc = near((1, 2), (orbitals, next_block), acc)
 
     share = width // occ_size
     piece_shape = jax.ShapeDtypeStruct((width, share), jnp.float32)

time: 38.7 us -> 38.7 us (level)
  no operation moved by 1% of the time
where the time goes in v2:
time: 38.7 us; the launch traced here: 38.6 us
  starting transfers between devices  14.8 us (38%)
  Pallas kernels  9.75 us (25%)
  waiting for transfers between devices  9.68 us (25%)
  local copies, waits for them, and re-layouts  1.81 us (5%)
  between operations  1.63 us (4%)
  other arithmetic  0.89 us (2%)
    ppermute x3, starting transfers between devices, per_device(): lax.ppermute(chunk, ('aux', 'occ'), aux_exchange(k, aux_size, occ_size))  5.29 us
    pallas_call x1, Pallas kernels, per_device(): pl.pallas_call(functools.partial(last_kernel, needed, occ_size), out_shap...  3.89 us
    ppermute x3, waiting for transfers between devices, per_device(): lax.ppermute(chunk, ('aux', 'occ'), aux_exchange(k, aux_size, occ_size))  3.83 us
    ppermute x3, starting transfers between devices, per_device(): lax.ppermute(sent, 'aux', exchange_pairs(k, aux_size))  3.68 us
    ppermute x3, waiting for transfers between devices, per_device(): lax.ppermute(sent, 'aux', exchange_pairs(k, aux_size))  3.1 us
    ppermute x1, starting transfers between devices, per_device(): next_block = lax.ppermute(orbitals, 'blk', exchange_pairs(1, blk_size))  3.05 us
    ppermute x1, starting transfers between devices, per_device(): parts.append(lax.ppermute(sent, ('aux', 'blk', 'occ'), pairs))  2.65 us
    pallas_call x2, Pallas kernels, near(): pl.pallas_call(functools.partial(near_kernel, groups), out_shape=acc_shap...  2.12 us
  transfers between devices with their start and end apart: 10, of which 6 were waited for; matrix products, arithmetic and copies ran while one was open for 0% of the time, Pallas kernels for 15%

profile of v2, /device:TPU:0, one launch (start us, length us, event | category | flops | bytes accessed | tf_op | source)
XLA Modules:
  0.0 38.6 jit_solution(16503901665920866621)
XLA Ops:
  0.0 3.1 %collective-permute-start.4 = (bf16[512,256]{1,0:T(8,128)(2,1)}, bf16[512,256]{1,0:T(8,128)(2,1)S(1)}, u32[]{:S(2)}, u32[]{:S(2)}) collective-permute-start(bf16[512,256]{1,0:T(8,128)(2,1)} %rest_0_.3), channel_id=1, source_target_pairs={{0,2},{2,0},{4,6},{6,4},{1,3},{3,1},{5,7},{7,5},{8,10},{10,8},{12,... | collective-permute-start | bytes 786440 | tf_op jit(solution)/shard_map/ppermute | solution.py:233
  3.1 1.1 %head.1 = bf16[256,256]{1,0:T(8,128)(2,1)S(1)} custom-call(bf16[512,256]{1,0:T(8,128)(2,1)} %rest_0_.3), custom_call_target="tpu_custom_call" | custom-call | flops 23622320128 | bytes 92274688 | tf_op jit(solution)/shard_map/head/pallas_call | solution.py:222
  4.1 0.0 copy-start.1
  4.1 2.7 %collective-permute-start = (bf16[256,256]{1,0:T(8,128)(2,1)S(1)}, bf16[256,256]{1,0:T(8,128)(2,1)S(1)}, u32[]{:S(2)}, u32[]{:S(2)}) collective-permute-start(bf16[256,256]{1,0:T(8,128)(2,1)S(1)} %head.1), channel_id=1, source_target_pairs={{0,4},{2,6},{4,0},{6,2},{1,5},{3,7},{5,1},{7,3},{8,12},{10,14},{12... | collective-permute-start | bytes 393224 | tf_op jit(solution)/shard_map/ppermute | solution.py:232
  8.2 0.8 %sort.1.table = s32[29]{0:T(128)S(4)} custom-call(s32[1]{0:T(128)S(6)} %copy.11.counts, s32[1,11]{1,0:T(1,128)S(1)} %copy-done.2), custom_call_target="tpu_custom_call" | custom-call | flops 536870912 | bytes 2097152 | tf_op jit(solution)/shard_map/sort/pallas_call | solution.py:241
  9.1 1.6 %copy-done = bf16[4,1,11,512,512]{4,3,2,1,0:T(8,128)(2,1)S(1)} copy-done((bf16[4,1,11,512,512]{4,3,2,1,0:T(8,128)(2,1)S(1)}, bf16[4,1,11,512,512]{4,3,2,1,0:T(8,128)(2,1)}, u32[]{:S(2)}) %copy-start) | copy-done | bytes 23068696
  10.7 0.2 copy-done.1
  10.9 1.4 %shard_map.46.rest_2_ = f32[4,512,256]{2,1,0:T(8,128)S(1)} custom-call(s32[29]{0:T(128)S(4)} %sort.1.table, bf16[4,1,11,512,512]{4,3,2,1,0:T(8,128)(2,1)S(1)} %copy-done, bf16[512,256]{1,0:T(8,128)(2,1)S(1)} %copy-done.1), custom_call_target="tpu_custom_call" | custom-call | flops 1073741824 | bytes 4194304 | tf_op jit(solution)/shard_map/pallas_call | solution.py:252
  12.3 0.0 collective-permute-done.rest_0_
  12.3 1.6 %collective-permute-start.1 = (bf16[256,256]{1,0:T(8,128)(2,1)S(1)}, bf16[256,256]{1,0:T(8,128)(2,1)S(1)}, u32[]{:S(2)}, u32[]{:S(2)}) collective-permute-start(bf16[256,256]{1,0:T(8,128)(2,1)S(1)} %collective-permute-done.rest_0_), channel_id=1, source_target_pairs={{0,8},{1,17},{8,0},{9,25},{16,24},{17,1},{24,16},{25,9},{2,10},{3,... | collective-permute-start | bytes 393224 | tf_op jit(solution)/shard_map/ppermute | solution.py:265
  13.9 3.7 %collective-permute-start.2 = (bf16[256,256]{1,0:T(8,128)(2,1)S(1)}, bf16[256,256]{1,0:T(8,128)(2,1)S(1)}, u32[]{:S(2)}, u32[]{:S(2)}) collective-permute-start(bf16[256,256]{1,0:T(8,128)(2,1)S(1)} %collective-permute-done.rest_0_), channel_id=1, source_target_pairs={{0,16},{1,9},{8,24},{9,1},{16,0},{17,25},{24,8},{25,17},{2,18},{3,... | collective-permute-start | bytes 393224 | tf_op jit(solution)/shard_map/ppermute | solution.py:265
  17.6 0.0 collective-permute-start.3
  17.6 0.0 collective-permute-done.4.rest_1_
  17.6 0.7 %shard_map.47.rest_2_ = f32[4,512,256]{2,1,0:T(8,128)S(1)} custom-call(s32[29]{0:T(128)S(4)} %sort.1.table, bf16[4,1,11,512,512]{4,3,2,1,0:T(8,128)(2,1)S(1)} %copy-done, bf16[512,256]{1,0:T(8,128)(2,1)S(1)} %copy-done.1, bf16[512,256]{1,0:T(8,128)(2,1)S(1)} %collective-permute-done.4.rest_1_, ...), custom_call_target="tpu_custom_call", output_to_operand_aliasing={{}: (4, {})} | custom-call | flops 1073741824 | bytes 4194304 | tf_op jit(solution)/shard_map/pallas_call | solution.py:252
  18.3 0.0 collective-permute-done.1.rest_1_
  18.3 1.3 %far.1.rest_4_ = f32[4,512,256]{2,1,0:T(8,128)S(1)} custom-call(s32[29]{0:T(128)S(4)} %sort.1.table, bf16[4,1,11,512,512]{4,3,2,1,0:T(8,128)(2,1)S(1)} %copy-done, bf16[256,256]{1,0:T(8,128)(2,1)S(1)} %collective-permute-done.rest_0_, bf16[256,256]{1,0:T(8,128)(2,1)S(1)} %collective-permute-done.1.rest_1_, ...), custom_call_target="tpu_custom_call", output_to_operand_aliasing={{}: (4, {})} | custom-call | flops 1610612736 | bytes 6291456 | tf_op jit(solution)/shard_map/far/pallas_call | solution.py:277
  19.6 2.3 %collective-permute-done.2.rest_2_ = bf16[256,256]{1,0:T(8,128)(2,1)S(1)} collective-permute-done((bf16[256,256]{1,0:T(8,128)(2,1)S(1)}, bf16[256,256]{1,0:T(8,128)(2,1)S(1)}, u32[]{:S(2)}, u32[]{:S(2)}) %collective-permute-start.2) | collective-permute-done | bytes 131104 | tf_op jit(solution)/shard_map/ppermute | solution.py:265
  21.9 1.5 %collective-permute-done.3.rest_3_ = bf16[256,256]{1,0:T(8,128)(2,1)S(1)} collective-permute-done((bf16[256,256]{1,0:T(8,128)(2,1)S(1)}, bf16[256,256]{1,0:T(8,128)(2,1)S(1)}, u32[]{:S(2)}, u32[]{:S(2)}) %collective-permute-start.3) | collective-permute-done | bytes 131104 | tf_op jit(solution)/shard_map/ppermute | solution.py:265
  23.4 3.9 %last.1 = (f32[4,512,256]{2,1,0:T(8,128)S(1)}, bf16[512,1024]{1,0:T(8,128)(2,1)S(1)}, f32[512,256]{1,0:T(8,128)S(1)}) custom-call(s32[29]{0:T(128)S(4)} %sort.1.table, bf16[4,1,11,512,512]{4,3,2,1,0:T(8,128)(2,1)S(1)} %copy-done, bf16[256,256]{1,0:T(8,128)(2,1)S(1)} %collective-permute-done.rest_0_, ...), custom_call_target="tpu_custom_call", output_to_operand_aliasing={{0}: (6, {})} | custom-call | flops 1610612736 | bytes 6291456 | tf_op jit(solution)/shard_map/last/pallas_call | solution.py:289
  27.4 0.1 collective-permute-start.5
  27.4 0.5 %kept.1.refs_0_ = f32[512,256]{1,0:T(8,128)S(1)} custom-call(bf16[512,1024]{1,0:T(8,128)(2,1)S(1)} %get-tuple-element.15.halves), custom_call_target="tpu_custom_call" | custom-call | flops 536870912 | bytes 2097152 | tf_op jit(solution)/shard_map/kept/pallas_call | solution.py:300
  27.9 1.4 %collective-permute-done.5.refs_1_ = f32[512,256]{1,0:T(8,128)S(1)} collective-permute-done((f32[512,256]{1,0:T(8,128)S(1)}, f32[512,256]{1,0:T(8,128)S(1)}, u32[]{:S(2)}, u32[]{:S(2)}) %collective-permute-start.5) | collective-permute-done | bytes 524320 | tf_op jit(solution)/shard_map/ppermute | solution.py:311
  29.3 0.1 split.1
  29.4 0.8 %collective-permute-start.6 = (f16[144,256]{1,0:T(8,128)(2,1)S(1)}, f16[144,256]{1,0:T(8,128)(2,1)S(1)}, u32[]{:S(2)}, u32[]{:S(2)}) collective-permute-start(f16[144,256]{1,0:T(8,128)(2,1)S(1)} %convert_element_type.18), channel_id=1, source_target_pairs={{0,8},{8,0},{16,24},{24,16},{1,9},{9,1},{17,25},{25,17},{2,10},{10... | collective-permute-start | bytes 221192 | tf_op jit(solution)/shard_map/ppermute | solution.py:326
  30.3 0.5 %collective-permute-start.7 = (f16[144,256]{1,0:T(8,128)(2,1)S(1)}, f16[144,256]{1,0:T(8,128)(2,1)S(1)}, u32[]{:S(2)}, u32[]{:S(2)}) collective-permute-start(f16[144,256]{1,0:T(8,128)(2,1)S(1)} %convert_element_type.20), channel_id=1, source_target_pairs={{0,16},{8,24},{16,0},{24,8},{1,17},{9,25},{17,1},{25,9},{2,18},{10... | collective-permute-start | bytes 221192 | tf_op jit(solution)/shard_map/ppermute | solution.py:326
  30.9 2.3 %collective-permute-start.8 = (f16[144,256]{1,0:T(8,128)(2,1)S(1)}, f16[144,256]{1,0:T(8,128)(2,1)S(1)}, u32[]{:S(2)}, u32[]{:S(2)}) collective-permute-start(f16[144,256]{1,0:T(8,128)(2,1)S(1)} %convert_element_type.22), channel_id=1, source_target_pairs={{0,24},{8,16},{16,8},{24,0},{1,25},{9,17},{17,9},{25,1},{2,26},{10... | collective-permute-start | bytes 221192 | tf_op jit(solution)/shard_map/ppermute | solution.py:326
  33.2 0.7 %collective-permute-done.6 = f16[144,256]{1,0:T(8,128)(2,1)S(1)} collective-permute-done((f16[144,256]{1,0:T(8,128)(2,1)S(1)}, f16[144,256]{1,0:T(8,128)(2,1)S(1)}, u32[]{:S(2)}, u32[]{:S(2)}) %collective-permute-start.6) | collective-permute-done | bytes 73760 | tf_op jit(solution)/shard_map/ppermute | solution.py:326
  33.9 2.4 %collective-permute-done.7 = f16[144,256]{1,0:T(8,128)(2,1)S(1)} collective-permute-done((f16[144,256]{1,0:T(8,128)(2,1)S(1)}, f16[144,256]{1,0:T(8,128)(2,1)S(1)}, u32[]{:S(2)}, u32[]{:S(2)}) %collective-permute-start.7) | collective-permute-done | bytes 73760 | tf_op jit(solution)/shard_map/ppermute | solution.py:326
  36.3 0.0 collective-permute-done.8
  36.4 0.1 collective-permute-start.9
  36.5 1.3 %collective-permute-done.9 = f32[128,256]{1,0:T(8,128)S(1)} collective-permute-done((f32[128,256]{1,0:T(8,128)S(1)}, f32[128,256]{1,0:T(8,128)S(1)}, u32[]{:S(2)}, u32[]{:S(2)}) %collective-permute-start.9) | collective-permute-done | bytes 131104 | tf_op jit(solution)/shard_map/ppermute | solution.py:329
  37.9 0.7 %maximum_bitcast_fusion = f32[1,128,512]{2,1,0:T(8,128)} fusion(f32[128,256]{1,0:T(8,128)S(1)} %get-tuple-element.22, f32[128,256]{1,0:T(8,128)S(1)} %get-tuple-element.21), kind=kLoop, calls=%fused_computation | loop fusion | flops 65536 | bytes 524288 | tf_op jit(solution)/shard_map/broadcast_in_dim | solution.py:337
  (14 shorter events, 0.2 us)
Async XLA Ops:
  0.0 8.2 %copy-start.2 = (s32[1,11]{1,0:T(1,128)S(1)}, s32[1,11]{1,0:T(1,128)}, u32[]{:S(2)}) copy-start(s32[1,11]{1,0:T(1,128)} %lists.1) | copy-start | bytes 136
  0.0 17.6 %collective-permute-start.4 = (bf16[512,256]{1,0:T(8,128)(2,1)}, bf16[512,256]{1,0:T(8,128)(2,1)S(1)}, u32[]{:S(2)}, u32[]{:S(2)}) collective-permute-start(bf16[512,256]{1,0:T(8,128)(2,1)} %rest_0_.3), channel_id=1, source_target_pairs={{0,2},{2,0},{4,6},{6,4},{1,3},{3,1},{5,7},{7,5},{8,10},{10,8},{12,... | collective-permute-start | bytes 786440 | tf_op jit(solution)/shard_map/ppermute | solution.py:233
  3.1 7.6 %copy-start = (bf16[4,1,11,512,512]{4,3,2,1,0:T(8,128)(2,1)S(1)}, bf16[4,1,11,512,512]{4,3,2,1,0:T(8,128)(2,1)}, u32[]{:S(2)}) copy-start(bf16[4,1,11,512,512]{4,3,2,1,0:T(8,128)(2,1)} %ints_ref.7) | copy-start | bytes 69206016
  4.1 6.7 %copy-start.1 = (bf16[512,256]{1,0:T(8,128)(2,1)S(1)}, bf16[512,256]{1,0:T(8,128)(2,1)}, u32[]{:S(2)}) copy-start(bf16[512,256]{1,0:T(8,128)(2,1)} %rest_0_.3) | copy-start | bytes 786436
  4.1 8.1 %collective-permute-start = (bf16[256,256]{1,0:T(8,128)(2,1)S(1)}, bf16[256,256]{1,0:T(8,128)(2,1)S(1)}, u32[]{:S(2)}, u32[]{:S(2)}) collective-permute-start(bf16[256,256]{1,0:T(8,128)(2,1)S(1)} %head.1), channel_id=1, source_target_pairs={{0,4},{2,6},{4,0},{6,2},{1,5},{3,7},{5,1},{7,3},{8,12},{10,14},{12... | collective-permute-start | bytes 393224 | tf_op jit(solution)/shard_map/ppermute | solution.py:232
  12.3 6.0 %collective-permute-start.1 = (bf16[256,256]{1,0:T(8,128)(2,1)S(1)}, bf16[256,256]{1,0:T(8,128)(2,1)S(1)}, u32[]{:S(2)}, u32[]{:S(2)}) collective-permute-start(bf16[256,256]{1,0:T(8,128)(2,1)S(1)} %collective-permute-done.rest_0_), channel_id=1, source_target_pairs={{0,8},{1,17},{8,0},{9,25},{16,24},{17,1},{24,16},{25,9},{2,10},{3,... | collective-permute-start | bytes 393224 | tf_op jit(solution)/shard_map/ppermute | solution.py:265
  13.9 8.1 %collective-permute-start.2 = (bf16[256,256]{1,0:T(8,128)(2,1)S(1)}, bf16[256,256]{1,0:T(8,128)(2,1)S(1)}, u32[]{:S(2)}, u32[]{:S(2)}) collective-permute-start(bf16[256,256]{1,0:T(8,128)(2,1)S(1)} %collective-permute-done.rest_0_), channel_id=1, source_target_pairs={{0,16},{1,9},{8,24},{9,1},{16,0},{17,25},{24,8},{25,17},{2,18},{3,... | collective-permute-start | bytes 393224 | tf_op jit(solution)/shard_map/ppermute | solution.py:265
  17.6 5.9 %collective-permute-start.3 = (bf16[256,256]{1,0:T(8,128)(2,1)S(1)}, bf16[256,256]{1,0:T(8,128)(2,1)S(1)}, u32[]{:S(2)}, u32[]{:S(2)}) collective-permute-start(bf16[256,256]{1,0:T(8,128)(2,1)S(1)} %collective-permute-done.rest_0_), channel_id=1, source_target_pairs={{0,24},{1,25},{8,16},{9,17},{16,8},{17,9},{24,0},{25,1},{2,26},{3,... | collective-permute-start | bytes 393224 | tf_op jit(solution)/shard_map/ppermute | solution.py:265
  27.4 2.0 %collective-permute-start.5 = (f32[512,256]{1,0:T(8,128)S(1)}, f32[512,256]{1,0:T(8,128)S(1)}, u32[]{:S(2)}, u32[]{:S(2)}) collective-permute-start(f32[512,256]{1,0:T(8,128)S(1)} %get-tuple-element.16), channel_id=1, source_target_pairs={{0,1},{1,0},{2,3},{3,2},{4,5},{5,4},{6,7},{7,6},{8,9},{9,8},{10,11... | collective-permute-start | bytes 1572872 | tf_op jit(solution)/shard_map/ppermute | solution.py:311
  29.4 4.4 %collective-permute-start.6 = (f16[144,256]{1,0:T(8,128)(2,1)S(1)}, f16[144,256]{1,0:T(8,128)(2,1)S(1)}, u32[]{:S(2)}, u32[]{:S(2)}) collective-permute-start(f16[144,256]{1,0:T(8,128)(2,1)S(1)} %convert_element_type.18), channel_id=1, source_target_pairs={{0,8},{8,0},{16,24},{24,16},{1,9},{9,1},{17,25},{25,17},{2,10},{10... | collective-permute-start | bytes 221192 | tf_op jit(solution)/shard_map/ppermute | solution.py:326
  30.3 6.0 %collective-permute-start.7 = (f16[144,256]{1,0:T(8,128)(2,1)S(1)}, f16[144,256]{1,0:T(8,128)(2,1)S(1)}, u32[]{:S(2)}, u32[]{:S(2)}) collective-permute-start(f16[144,256]{1,0:T(8,128)(2,1)S(1)} %convert_element_type.20), channel_id=1, source_target_pairs={{0,16},{8,24},{16,0},{24,8},{1,17},{9,25},{17,1},{25,9},{2,18},{10... | collective-permute-start | bytes 221192 | tf_op jit(solution)/shard_map/ppermute | solution.py:326
  30.9 5.5 %collective-permute-start.8 = (f16[144,256]{1,0:T(8,128)(2,1)S(1)}, f16[144,256]{1,0:T(8,128)(2,1)S(1)}, u32[]{:S(2)}, u32[]{:S(2)}) collective-permute-start(f16[144,256]{1,0:T(8,128)(2,1)S(1)} %convert_element_type.22), channel_id=1, source_target_pairs={{0,24},{8,16},{16,8},{24,0},{1,25},{9,17},{17,9},{25,1},{2,26},{10... | collective-permute-start | bytes 221192 | tf_op jit(solution)/shard_map/ppermute | solution.py:326
  36.4 1.4 %collective-permute-start.9 = (f32[128,256]{1,0:T(8,128)S(1)}, f32[128,256]{1,0:T(8,128)S(1)}, u32[]{:S(2)}, u32[]{:S(2)}) collective-permute-start(f32[128,256]{1,0:T(8,128)S(1)} %fusion.1), channel_id=1, source_target_pairs={{0,1},{1,0},{2,3},{3,2},{4,5},{5,4},{6,7},{7,6},{8,9},{9,8},{10,11... | collective-permute-start | bytes 393224 | tf_op jit(solution)/shard_map/ppermute | solution.py:329

commit v3 on v1

--- a/solution.py
+++ b/solution.py
@@ -187,11 +187,24 @@
     return block[:depth] * jnp.exp2(block[depth : depth + 1] - SCALED_TOP)
 
 
+def join_kernel(*refs):
+    *shares, out_ref, sems = refs
+    width = shares[0].shape[1]
+    copies = []
+    for k, share in enumerate(shares):
+        start = (lax.axis_index("occ") ^ k) * width
+        columns = pl.ds(pl.multiple_of(start, width), width)
+        copies.append(pltpu.make_async_copy(share, out_ref.at[0, :, columns], sems.at[k]))
+    for copy in copies:
+        copy.start()
+    for copy in copies:
+        copy.wait()
+
+
 def per_device(integrals, orbitals, pair_lists, pair_counts):
     aux_total, _, slot_total, width, _ = integrals.shape
     columns = orbitals.shape[1]
     aux_size, blk_size, occ_size = (lax.axis_size(n) for n in ("aux", "blk", "occ"))
-    my_occ = lax.axis_index("occ")
     slot_flops = 2 * aux_total * width * width * columns
     slot_bytes = 2 * aux_total * width * width
 
@@ -321,13 +334,15 @@
     shares = [total] + [
         lax.ppermute(total, "occ", exchange_pairs(k, occ_size)) for k in range(1, occ_size)
     ]
-    ordered = []
-    for o in range(occ_size):
-        value = shares[0]
-        for k in range(1, occ_size):
-            value = jnp.where((my_occ ^ k) == o, shares[k], value)
-        ordered.append(value)
-    return jnp.concatenate(ordered, 1)[None]
+    return pl.pallas_call(
+        join_kernel,
+        out_shape=jax.ShapeDtypeStruct((1, rows, width), jnp.float32),
+        in_specs=[VMEM] * occ_size,
+        out_specs=HBM,
+        scratch_shapes=[pltpu.SemaphoreType.DMA((occ_size,))],
+        compiler_params=pltpu.CompilerParams(vmem_limit_bytes=1 << 20),
+        name="join",
+    )(*shares)
 
 
 def solution(mesh):

time: 38.7 us -> 39.7 us (1.026)
  waiting for transfers between devices: 9.68 us -> 10.8 us
  other arithmetic: 0.89 us -> 0.14 us
  Pallas kernels: 9.71 us -> 10.4 us
    broadcast_in_dim x1 -> x0, other arithmetic: 0.73 us -> none  [per_device(): return jnp.concatenate(ordered, 1)[None]]
    pallas_call x0 -> x1, Pallas kernels: none -> 0.71 us  [per_device(): pl.pallas_call(join_kernel, out_shape=jax.ShapeDtypeStruct((1, rows, widt...]
    ppermute x3, waiting for transfers between devices: 3.1 us -> 3.75 us  [per_device(): lax.ppermute(sent, 'aux', exchange_pairs(k, aux_size))]
    ppermute x3, waiting for transfers between devices: 3.83 us -> 4.31 us  [per_device(): lax.ppermute(chunk, ('aux', 'occ'), aux_exchange(k, aux_size, occ_size))]
  transfers between devices with their start and end apart: 10 -> 10, of which waited for: 6 -> 7; matrix products, arithmetic and copies ran while one was open for 0% -> 0% of each run, Pallas kernels for 15% -> 14%
where the time goes in v3:
time: 39.7 us; the launch traced here: 39.6 us
  starting transfers between devices  14.8 us (37%)
  waiting for transfers between devices  10.8 us (27%)
  Pallas kernels  10.4 us (26%)
  local copies, waits for them, and re-layouts  1.85 us (5%)
  between operations  1.61 us (4%)
    ppermute x3, starting transfers between devices, per_device(): lax.ppermute(chunk, ('aux', 'occ'), aux_exchange(k, aux_size, occ_size))  5.29 us
    ppermute x3, waiting for transfers between devices, per_device(): lax.ppermute(chunk, ('aux', 'occ'), aux_exchange(k, aux_size, occ_size))  4.31 us
    pallas_call x1, Pallas kernels, per_device(): pl.pallas_call(functools.partial(last_kernel, needed, occ_size), out_shap...  3.9 us
    ppermute x3, waiting for transfers between devices, per_device(): lax.ppermute(sent, 'aux', exchange_pairs(k, aux_size))  3.75 us
    ppermute x3, starting transfers between devices, per_device(): lax.ppermute(sent, 'aux', exchange_pairs(k, aux_size))  3.62 us
    ppermute x1, starting transfers between devices, per_device(): next_block = lax.ppermute(orbitals, 'blk', exchange_pairs(1, blk_size))  3.05 us
    ppermute x1, starting transfers between devices, per_device(): parts.append(lax.ppermute(sent, ('aux', 'blk', 'occ'), pairs))  2.65 us
    pallas_call x2, Pallas kernels, near(): pl.pallas_call(functools.partial(near_kernel, group), out_shape=acc_shape...  2.12 us
  transfers between devices with their start and end apart: 10, of which 7 were waited for; matrix products, arithmetic and copies ran while one was open for 0% of the time, Pallas kernels for 14%

profile of v3, /device:TPU:0, one launch (start us, length us, event | category | flops | bytes accessed | tf_op | source)
XLA Modules:
  0.0 39.6 jit_solution(418980014397583152)
XLA Ops:
  0.0 3.1 %collective-permute-start.4 = (bf16[512,256]{1,0:T(8,128)(2,1)}, bf16[512,256]{1,0:T(8,128)(2,1)S(1)}, u32[]{:S(2)}, u32[]{:S(2)}) collective-permute-start(bf16[512,256]{1,0:T(8,128)(2,1)} %coef_ref.1), channel_id=1, source_target_pairs={{0,2},{2,0},{4,6},{6,4},{1,3},{3,1},{5,7},{7,5},{8,10},{10,8},{12,... | collective-permute-start | bytes 786440 | tf_op jit(solution)/shard_map/ppermute | solution.py:239
  3.1 1.1 %head.1 = bf16[256,256]{1,0:T(8,128)(2,1)S(1)} custom-call(bf16[512,256]{1,0:T(8,128)(2,1)} %coef_ref.1), custom_call_target="tpu_custom_call" | custom-call | flops 23622320128 | bytes 92274688 | tf_op jit(solution)/shard_map/head/pallas_call | solution.py:228
  4.1 0.0 copy-start.1
  4.1 2.7 %collective-permute-start = (bf16[256,256]{1,0:T(8,128)(2,1)S(1)}, bf16[256,256]{1,0:T(8,128)(2,1)S(1)}, u32[]{:S(2)}, u32[]{:S(2)}) collective-permute-start(bf16[256,256]{1,0:T(8,128)(2,1)S(1)} %head.1), channel_id=1, source_target_pairs={{0,4},{2,6},{4,0},{6,2},{1,5},{3,7},{5,1},{7,3},{8,12},{10,14},{12... | collective-permute-start | bytes 393224 | tf_op jit(solution)/shard_map/ppermute | solution.py:238
  8.2 0.8 %sort.1.table = s32[28]{0:T(128)S(4)} custom-call(s32[1]{0:T(128)S(6)} %copy.11.counts, s32[1,11]{1,0:T(1,128)S(1)} %copy-done.2), custom_call_target="tpu_custom_call" | custom-call | flops 536870912 | bytes 2097152 | tf_op jit(solution)/shard_map/sort/pallas_call | solution.py:247
  9.0 1.7 %copy-done = bf16[4,1,11,512,512]{4,3,2,1,0:T(8,128)(2,1)S(1)} copy-done((bf16[4,1,11,512,512]{4,3,2,1,0:T(8,128)(2,1)S(1)}, bf16[4,1,11,512,512]{4,3,2,1,0:T(8,128)(2,1)}, u32[]{:S(2)}) %copy-start) | copy-done | bytes 23068696
  10.7 0.2 copy-done.1
  10.9 1.4 %shard_map.46.accs_0_ = f32[4,512,256]{2,1,0:T(8,128)S(1)} custom-call(s32[28]{0:T(128)S(4)} %sort.1.table, bf16[4,1,11,512,512]{4,3,2,1,0:T(8,128)(2,1)S(1)} %copy-done, bf16[512,256]{1,0:T(8,128)(2,1)S(1)} %copy-done.1), custom_call_target="tpu_custom_call" | custom-call | flops 1073741824 | bytes 4194304 | tf_op jit(solution)/shard_map/pallas_call | solution.py:258
  12.3 0.0 collective-permute-done.rest_0_
  12.3 1.6 %collective-permute-start.1 = (bf16[256,256]{1,0:T(8,128)(2,1)S(1)}, bf16[256,256]{1,0:T(8,128)(2,1)S(1)}, u32[]{:S(2)}, u32[]{:S(2)}) collective-permute-start(bf16[256,256]{1,0:T(8,128)(2,1)S(1)} %collective-permute-done.rest_0_), channel_id=1, source_target_pairs={{0,8},{1,17},{8,0},{9,25},{16,24},{17,1},{24,16},{25,9},{2,10},{3,... | collective-permute-start | bytes 393224 | tf_op jit(solution)/shard_map/ppermute | solution.py:271
  13.9 3.7 %collective-permute-start.3 = (bf16[256,256]{1,0:T(8,128)(2,1)S(1)}, bf16[256,256]{1,0:T(8,128)(2,1)S(1)}, u32[]{:S(2)}, u32[]{:S(2)}) collective-permute-start(bf16[256,256]{1,0:T(8,128)(2,1)S(1)} %collective-permute-done.rest_0_), channel_id=1, source_target_pairs={{0,24},{1,25},{8,16},{9,17},{16,8},{17,9},{24,0},{25,1},{2,26},{3,... | collective-permute-start | bytes 393224 | tf_op jit(solution)/shard_map/ppermute | solution.py:271
  17.6 0.0 collective-permute-start.2
  17.6 0.0 collective-permute-done.4.coef_ref
  17.6 0.7 %shard_map.47.rest_2_ = f32[4,512,256]{2,1,0:T(8,128)S(1)} custom-call(s32[28]{0:T(128)S(4)} %sort.1.table, bf16[4,1,11,512,512]{4,3,2,1,0:T(8,128)(2,1)S(1)} %copy-done, bf16[512,256]{1,0:T(8,128)(2,1)S(1)} %collective-permute-done.4.coef_ref, f32[4,512,256]{2,1,0:T(8,128)S(1)} %shard_map.46.accs_0_), custom_call_target="tpu_custom_call", output_to_operand_aliasing={{}: (3, {})} | custom-call | flops 1073741824 | bytes 4194304 | tf_op jit(solution)/shard_map/pallas_call | solution.py:258
  18.3 0.0 collective-permute-done.1.rest_1_
  18.3 1.3 %far.1.rest_4_ = f32[4,512,256]{2,1,0:T(8,128)S(1)} custom-call(s32[28]{0:T(128)S(4)} %sort.1.table, bf16[4,1,11,512,512]{4,3,2,1,0:T(8,128)(2,1)S(1)} %copy-done, bf16[256,256]{1,0:T(8,128)(2,1)S(1)} %collective-permute-done.rest_0_, bf16[256,256]{1,0:T(8,128)(2,1)S(1)} %collective-permute-done.1.rest_1_, ...), custom_call_target="tpu_custom_call", output_to_operand_aliasing={{}: (4, {})} | custom-call | flops 1610612736 | bytes 6291456 | tf_op jit(solution)/shard_map/far/pallas_call | solution.py:283
  19.6 3.8 %collective-permute-done.3.rest_3_ = bf16[256,256]{1,0:T(8,128)(2,1)S(1)} collective-permute-done((bf16[256,256]{1,0:T(8,128)(2,1)S(1)}, bf16[256,256]{1,0:T(8,128)(2,1)S(1)}, u32[]{:S(2)}, u32[]{:S(2)}) %collective-permute-start.3) | collective-permute-done | bytes 131104 | tf_op jit(solution)/shard_map/ppermute | solution.py:271
  23.4 0.5 %collective-permute-done.2.rest_2_ = bf16[256,256]{1,0:T(8,128)(2,1)S(1)} collective-permute-done((bf16[256,256]{1,0:T(8,128)(2,1)S(1)}, bf16[256,256]{1,0:T(8,128)(2,1)S(1)}, u32[]{:S(2)}, u32[]{:S(2)}) %collective-permute-start.2) | collective-permute-done | bytes 131104 | tf_op jit(solution)/shard_map/ppermute | solution.py:271
  23.9 3.9 %last.1 = (f32[4,512,256]{2,1,0:T(8,128)S(1)}, bf16[512,1024]{1,0:T(8,128)(2,1)S(1)}, f32[512,256]{1,0:T(8,128)S(1)}) custom-call(s32[28]{0:T(128)S(4)} %sort.1.table, bf16[4,1,11,512,512]{4,3,2,1,0:T(8,128)(2,1)S(1)} %copy-done, bf16[256,256]{1,0:T(8,128)(2,1)S(1)} %collective-permute-done.rest_0_, ...), custom_call_target="tpu_custom_call", output_to_operand_aliasing={{0}: (6, {})} | custom-call | flops 1610612736 | bytes 6291456 | tf_op jit(solution)/shard_map/last/pallas_call | solution.py:295
  27.8 0.1 collective-permute-start.5
  27.9 0.5 %kept.1.refs_0_ = f32[512,256]{1,0:T(8,128)S(1)} custom-call(bf16[512,1024]{1,0:T(8,128)(2,1)S(1)} %get-tuple-element.15.halves), custom_call_target="tpu_custom_call" | custom-call | flops 536870912 | bytes 2097152 | tf_op jit(solution)/shard_map/kept/pallas_call | solution.py:306
  28.4 1.4 %collective-permute-done.5.refs_1_ = f32[512,256]{1,0:T(8,128)S(1)} collective-permute-done((f32[512,256]{1,0:T(8,128)S(1)}, f32[512,256]{1,0:T(8,128)S(1)}, u32[]{:S(2)}, u32[]{:S(2)}) %collective-permute-start.5) | collective-permute-done | bytes 524320 | tf_op jit(solution)/shard_map/ppermute | solution.py:317
  29.8 0.1 split.1
  29.9 0.9 %collective-permute-start.8 = (f16[144,256]{1,0:T(8,128)(2,1)S(1)}, f16[144,256]{1,0:T(8,128)(2,1)S(1)}, u32[]{:S(2)}, u32[]{:S(2)}) collective-permute-start(f16[144,256]{1,0:T(8,128)(2,1)S(1)} %convert_element_type.22), channel_id=1, source_target_pairs={{0,24},{8,16},{16,8},{24,0},{1,25},{9,17},{17,9},{25,1},{2,26},{10... | collective-permute-start | bytes 221192 | tf_op jit(solution)/shard_map/ppermute | solution.py:332
  30.8 2.2 %collective-permute-start.7 = (f16[144,256]{1,0:T(8,128)(2,1)S(1)}, f16[144,256]{1,0:T(8,128)(2,1)S(1)}, u32[]{:S(2)}, u32[]{:S(2)}) collective-permute-start(f16[144,256]{1,0:T(8,128)(2,1)S(1)} %convert_element_type.20), channel_id=1, source_target_pairs={{0,16},{8,24},{16,0},{24,8},{1,17},{9,25},{17,1},{25,9},{2,18},{10... | collective-permute-start | bytes 221192 | tf_op jit(solution)/shard_map/ppermute | solution.py:332
  33.0 0.5 %collective-permute-start.6 = (f16[144,256]{1,0:T(8,128)(2,1)S(1)}, f16[144,256]{1,0:T(8,128)(2,1)S(1)}, u32[]{:S(2)}, u32[]{:S(2)}) collective-permute-start(f16[144,256]{1,0:T(8,128)(2,1)S(1)} %convert_element_type.18), channel_id=1, source_target_pairs={{0,8},{8,0},{16,24},{24,16},{1,9},{9,1},{17,25},{25,17},{2,10},{10... | collective-permute-start | bytes 221192 | tf_op jit(solution)/shard_map/ppermute | solution.py:332
  33.6 1.9 %collective-permute-done.8 = f16[144,256]{1,0:T(8,128)(2,1)S(1)} collective-permute-done((f16[144,256]{1,0:T(8,128)(2,1)S(1)}, f16[144,256]{1,0:T(8,128)(2,1)S(1)}, u32[]{:S(2)}, u32[]{:S(2)}) %collective-permute-start.8) | collective-permute-done | bytes 73760 | tf_op jit(solution)/shard_map/ppermute | solution.py:332
  35.5 1.3 %collective-permute-done.7 = f16[144,256]{1,0:T(8,128)(2,1)S(1)} collective-permute-done((f16[144,256]{1,0:T(8,128)(2,1)S(1)}, f16[144,256]{1,0:T(8,128)(2,1)S(1)}, u32[]{:S(2)}, u32[]{:S(2)}) %collective-permute-start.7) | collective-permute-done | bytes 73760 | tf_op jit(solution)/shard_map/ppermute | solution.py:332
  36.8 0.6 %collective-permute-done.6 = f16[144,256]{1,0:T(8,128)(2,1)S(1)} collective-permute-done((f16[144,256]{1,0:T(8,128)(2,1)S(1)}, f16[144,256]{1,0:T(8,128)(2,1)S(1)}, u32[]{:S(2)}, u32[]{:S(2)}) %collective-permute-start.6) | collective-permute-done | bytes 73760 | tf_op jit(solution)/shard_map/ppermute | solution.py:332
  37.5 0.1 collective-permute-start.9
  37.5 1.3 %collective-permute-done.9.refs_1_ = f32[128,256]{1,0:T(8,128)S(1)} collective-permute-done((f32[128,256]{1,0:T(8,128)S(1)}, f32[128,256]{1,0:T(8,128)S(1)}, u32[]{:S(2)}, u32[]{:S(2)}) %collective-permute-start.9) | collective-permute-done | bytes 131104 | tf_op jit(solution)/shard_map/ppermute | solution.py:335
  38.9 0.7 %join.1 = f32[1,128,512]{2,1,0:T(8,128)} custom-call(f32[128,256]{1,0:T(8,128)S(1)} %fusion.1.refs_0_, f32[128,256]{1,0:T(8,128)S(1)} %collective-permute-done.9.refs_1_), custom_call_target="tpu_custom_call" | custom-call | tf_op jit(solution)/shard_map/join/pallas_call | solution.py:337
  (13 shorter events, 0.1 us)
Async XLA Ops:
  0.0 8.2 %copy-start.2 = (s32[1,11]{1,0:T(1,128)S(1)}, s32[1,11]{1,0:T(1,128)}, u32[]{:S(2)}) copy-start(s32[1,11]{1,0:T(1,128)} %lists.1) | copy-start | bytes 136
  0.0 17.6 %collective-permute-start.4 = (bf16[512,256]{1,0:T(8,128)(2,1)}, bf16[512,256]{1,0:T(8,128)(2,1)S(1)}, u32[]{:S(2)}, u32[]{:S(2)}) collective-permute-start(bf16[512,256]{1,0:T(8,128)(2,1)} %coef_ref.1), channel_id=1, source_target_pairs={{0,2},{2,0},{4,6},{6,4},{1,3},{3,1},{5,7},{7,5},{8,10},{10,8},{12,... | collective-permute-start | bytes 786440 | tf_op jit(solution)/shard_map/ppermute | solution.py:239
  3.1 7.6 %copy-start = (bf16[4,1,11,512,512]{4,3,2,1,0:T(8,128)(2,1)S(1)}, bf16[4,1,11,512,512]{4,3,2,1,0:T(8,128)(2,1)}, u32[]{:S(2)}) copy-start(bf16[4,1,11,512,512]{4,3,2,1,0:T(8,128)(2,1)} %ints_ref.7) | copy-start | bytes 69206016
  4.1 6.7 %copy-start.1 = (bf16[512,256]{1,0:T(8,128)(2,1)S(1)}, bf16[512,256]{1,0:T(8,128)(2,1)}, u32[]{:S(2)}) copy-start(bf16[512,256]{1,0:T(8,128)(2,1)} %coef_ref.1) | copy-start | bytes 786436
  4.1 8.1 %collective-permute-start = (bf16[256,256]{1,0:T(8,128)(2,1)S(1)}, bf16[256,256]{1,0:T(8,128)(2,1)S(1)}, u32[]{:S(2)}, u32[]{:S(2)}) collective-permute-start(bf16[256,256]{1,0:T(8,128)(2,1)S(1)} %head.1), channel_id=1, source_target_pairs={{0,4},{2,6},{4,0},{6,2},{1,5},{3,7},{5,1},{7,3},{8,12},{10,14},{12... | collective-permute-start | bytes 393224 | tf_op jit(solution)/shard_map/ppermute | solution.py:238
  12.3 6.0 %collective-permute-start.1 = (bf16[256,256]{1,0:T(8,128)(2,1)S(1)}, bf16[256,256]{1,0:T(8,128)(2,1)S(1)}, u32[]{:S(2)}, u32[]{:S(2)}) collective-permute-start(bf16[256,256]{1,0:T(8,128)(2,1)S(1)} %collective-permute-done.rest_0_), channel_id=1, source_target_pairs={{0,8},{1,17},{8,0},{9,25},{16,24},{17,1},{24,16},{25,9},{2,10},{3,... | collective-permute-start | bytes 393224 | tf_op jit(solution)/shard_map/ppermute | solution.py:271
  13.9 9.5 %collective-permute-start.3 = (bf16[256,256]{1,0:T(8,128)(2,1)S(1)}, bf16[256,256]{1,0:T(8,128)(2,1)S(1)}, u32[]{:S(2)}, u32[]{:S(2)}) collective-permute-start(bf16[256,256]{1,0:T(8,128)(2,1)S(1)} %collective-permute-done.rest_0_), channel_id=1, source_target_pairs={{0,24},{1,25},{8,16},{9,17},{16,8},{17,9},{24,0},{25,1},{2,26},{3,... | collective-permute-start | bytes 393224 | tf_op jit(solution)/shard_map/ppermute | solution.py:271
  17.6 6.4 %collective-permute-start.2 = (bf16[256,256]{1,0:T(8,128)(2,1)S(1)}, bf16[256,256]{1,0:T(8,128)(2,1)S(1)}, u32[]{:S(2)}, u32[]{:S(2)}) collective-permute-start(bf16[256,256]{1,0:T(8,128)(2,1)S(1)} %collective-permute-done.rest_0_), channel_id=1, source_target_pairs={{0,16},{1,9},{8,24},{9,1},{16,0},{17,25},{24,8},{25,17},{2,18},{3,... | collective-permute-start | bytes 393224 | tf_op jit(solution)/shard_map/ppermute | solution.py:271
  27.8 2.0 %collective-permute-start.5 = (f32[512,256]{1,0:T(8,128)S(1)}, f32[512,256]{1,0:T(8,128)S(1)}, u32[]{:S(2)}, u32[]{:S(2)}) collective-permute-start(f32[512,256]{1,0:T(8,128)S(1)} %get-tuple-element.16), channel_id=1, source_target_pairs={{0,1},{1,0},{2,3},{3,2},{4,5},{5,4},{6,7},{7,6},{8,9},{9,8},{10,11... | collective-permute-start | bytes 1572872 | tf_op jit(solution)/shard_map/ppermute | solution.py:317
  29.9 5.6 %collective-permute-start.8 = (f16[144,256]{1,0:T(8,128)(2,1)S(1)}, f16[144,256]{1,0:T(8,128)(2,1)S(1)}, u32[]{:S(2)}, u32[]{:S(2)}) collective-permute-start(f16[144,256]{1,0:T(8,128)(2,1)S(1)} %convert_element_type.22), channel_id=1, source_target_pairs={{0,24},{8,16},{16,8},{24,0},{1,25},{9,17},{17,9},{25,1},{2,26},{10... | collective-permute-start | bytes 221192 | tf_op jit(solution)/shard_map/ppermute | solution.py:332
  30.8 6.0 %collective-permute-start.7 = (f16[144,256]{1,0:T(8,128)(2,1)S(1)}, f16[144,256]{1,0:T(8,128)(2,1)S(1)}, u32[]{:S(2)}, u32[]{:S(2)}) collective-permute-start(f16[144,256]{1,0:T(8,128)(2,1)S(1)} %convert_element_type.20), channel_id=1, source_target_pairs={{0,16},{8,24},{16,0},{24,8},{1,17},{9,25},{17,1},{25,9},{2,18},{10... | collective-permute-start | bytes 221192 | tf_op jit(solution)/shard_map/ppermute | solution.py:332
  33.0 4.4 %collective-permute-start.6 = (f16[144,256]{1,0:T(8,128)(2,1)S(1)}, f16[144,256]{1,0:T(8,128)(2,1)S(1)}, u32[]{:S(2)}, u32[]{:S(2)}) collective-permute-start(f16[144,256]{1,0:T(8,128)(2,1)S(1)} %convert_element_type.18), channel_id=1, source_target_pairs={{0,8},{8,0},{16,24},{24,16},{1,9},{9,1},{17,25},{25,17},{2,10},{10... | collective-permute-start | bytes 221192 | tf_op jit(solution)/shard_map/ppermute | solution.py:332
  37.5 1.4 %collective-permute-start.9 = (f32[128,256]{1,0:T(8,128)S(1)}, f32[128,256]{1,0:T(8,128)S(1)}, u32[]{:S(2)}, u32[]{:S(2)}) collective-permute-start(f32[128,256]{1,0:T(8,128)S(1)} %fusion.1.refs_0_), channel_id=1, source_target_pairs={{0,1},{1,0},{2,3},{3,2},{4,5},{5,4},{6,7},{7,6},{8,9},{9,8},{10,11... | collective-permute-start | bytes 393224 | tf_op jit(solution)/shard_map/ppermute | solution.py:335
